TPU v7x, 512 devices: a whole 4x8x8 slice. The times are simulated.
512 devices in a mesh: lat: 16 (over x, y_lo), lon: 32 (over z, y_hi, core).
Axes of the slice: x: 4, y: 8 (y_hi: 2, y_lo: 4; y = y_hi * 4 + y_lo), z: 8, core: 2. Of those that a mesh axis runs over, the one named last changes fastest.
Arguments:
- ensemble: float32 [64, 256, 1792], P('lat', 'lon'), may hold values from -6 to 6
- northward_wind: float32 [64, 256], P('lat', 'lon'), may hold values from -1 to 1
- eastward_wind: float32 [64, 256], P('lat', 'lon'), may hold values from -1 to 1
- spreading_strength: float32 [64, 256], P('lat', 'lon'), may hold values from 0.05 to 0.2
- measurement_home_subdomain: int32 [3, 512], replicated, may hold values from 0 to 511, as said below
- obs_site: int32 [3, 512], replicated, may hold values from 0 to 895
- obs_class: int32 [3, 512], replicated, may hold values from 0 to 7
- cutoff_table: int32 [8], replicated, may hold values from 6 to 23
- obs_value: float32 [3, 512], replicated, may hold values from -6 to 6
- obs_var: float32 [3, 512], replicated, may hold values from 0.5 to 2
- obs_noise: float32 [3, 512, 64], replicated, may hold values from -6 to 6
Outputs:
- analysis: float32 [64, 256, 1792], P('lat', 'lon')
Inputs may be any that keep to these rules, and one draw needn't show every extreme that they name: `measurement_home_subdomain`: tile index is lat index * 32 + lon index; in every batch no tile owns more than 4 observations and some tile owns exactly 4.
All inputs are finite; a program needn't handle non-finite values.
Results may differ from a plain program's by a relative error of at most 0.0003.
Values sent between devices are 32-bit elements; how exact they have to be, the bound alone decides.
No kernel may reach another device: no remote copies, remote signals or barrier semaphores. Data moves between devices by JAX's collectives and lax.ppermute only.
A program may use at most 64 MiB of HBM per device.

v0:
```python
import jax
import jax.numpy as jnp
from jax import lax
from jax.sharding import PartitionSpec as P

LEV = 28
MEMBERS = 64
SECTIONS = 2
BATCH_GROUPS = 3


advect_coef = 0.2


def with_halo(block, sides, width, periodic):
    for axis, dim in sides:
        count = lax.axis_size(axis)
        forward = [(i, i + 1) for i in range(count - 1)]
        if periodic:
            forward.append((count - 1, 0))
        backward = [(target, source) for source, target in forward]
        low = lax.ppermute(
            lax.slice_in_dim(block, block.shape[dim] - width, None, axis=dim), axis, forward
        )
        high = lax.ppermute(lax.slice_in_dim(block, 0, width, axis=dim), axis, backward)
        block = jnp.concatenate([low, block, high], axis=dim)
    return block


def taper(dist, radius):
    z = dist / radius
    inner = 1.0 - 5.0 / 3.0 * z**2 + 0.625 * z**3 + 0.5 * z**4 - 0.25 * z**5
    outside = jnp.maximum(z, 1.0)
    outer = (
        4.0
        - 5.0 * outside
        + 5.0 / 3.0 * outside**2
        + 0.625 * outside**3
        - 0.5 * outside**4
        + outside**5 / 12.0
        - 2.0 / (3.0 * outside)
    )
    return jnp.where(z <= 1.0, inner, jnp.where(z < 2.0, outer, jnp.float32(0.0)))


def advance_subdomains(prognostic_fields, northward_wind, eastward_wind, spreading_strength):
    padded_lat = with_halo(prognostic_fields, (("lat", 0),), 1, False)
    padded_lon = with_halo(prognostic_fields, (("lon", 1),), 1, True)
    north = padded_lat[2:]
    south = padded_lat[:-2]
    east = padded_lon[:, 2:]
    west = padded_lon[:, :-2]
    lap = north + south + east + west - 4.0 * prognostic_fields
    return (
        prognostic_fields
        + spreading_strength[:, :, None] * lap
        - advect_coef
        * (northward_wind[:, :, None] * (north - south) + eastward_wind[:, :, None] * (east - west))
    )


def whiten(prior, value, var, noise):
    mean = jnp.mean(prior, axis=1, keepdims=True)
    anom = prior - mean
    cov = jnp.dot(anom, anom.T, precision=lax.Precision.HIGHEST) / jnp.float32(
        MEMBERS - 1
    ) + jnp.diag(var)
    factor = jnp.linalg.cholesky(cov)
    rhs = value[:, None] + jnp.sqrt(var)[:, None] * noise - prior
    return (anom, jax.scipy.linalg.cho_solve((factor, True), rhs))


def body(
    ensemble,
    northward_wind,
    eastward_wind,
    spreading_strength,
    measurement_home_subdomain,
    obs_site,
    obs_class,
    cutoff_table,
    obs_value,
    obs_var,
    obs_noise,
):
    tile_lat = ensemble.shape[0]
    tile_lon = ensemble.shape[1]
    lon_tiles = lax.axis_size("lon")
    lon_cells = tile_lon * lon_tiles
    row_base = lax.axis_index("lat") * tile_lat
    leading_column_offset = lax.axis_index("lon") * tile_lon
    myself = lax.axis_index("lat") * lon_tiles + lax.axis_index("lon")
    count = measurement_home_subdomain.shape[1]
    block = min(count, 128)
    prognostic_fields = ensemble
    for section in range(SECTIONS):
        prognostic_fields = advance_subdomains(
            prognostic_fields, northward_wind, eastward_wind, spreading_strength
        )
    lat_cells = row_base + jnp.arange(tile_lat, dtype=jnp.int32)
    lon_local = leading_column_offset + jnp.arange(tile_lon, dtype=jnp.int32)
    classes = jnp.arange(cutoff_table.shape[0], dtype=jnp.int32)
    for k in range(BATCH_GROUPS):
        owner = measurement_home_subdomain[k]
        site = obs_site[k]
        cell = site // LEV
        glat = owner // lon_tiles * tile_lat + cell // tile_lon
        glon = owner % lon_tiles * tile_lon + cell % tile_lon
        flat = prognostic_fields.reshape(-1, MEMBERS)
        picked = jnp.take(flat, site, axis=0)
        mine = owner == myself
        prior = lax.psum(jnp.where(mine[:, None], picked, jnp.float32(0.0)), ("lat", "lon"))
        anom_obs, white = whiten(prior, obs_value[k], obs_var[k], obs_noise[k])
        match = (obs_class[k][:, None] == classes[None, :]).astype(jnp.int32)
        radius = jnp.sum(match * cutoff_table[None, :], axis=1).astype(jnp.float32)
        dlat = jnp.abs(lat_cells[:, None] - glat[None, :]).astype(jnp.float32)
        dlon = jnp.abs(lon_local[:, None] - glon[None, :])
        dlon = jnp.minimum(dlon, lon_cells - dlon).astype(jnp.float32)
        dist = jnp.sqrt(dlat[:, None, :] * dlat[:, None, :] + dlon[None, :, :] * dlon[None, :, :])
        rho = taper(dist, radius[None, None, :]).reshape(tile_lat * tile_lon, count)
        cube = prognostic_fields.reshape(tile_lat * tile_lon, LEV, MEMBERS)
        xp = cube - jnp.mean(cube, axis=2, keepdims=True)
        total = jnp.zeros_like(cube)
        for start in range(0, count, block):
            part_anom = anom_obs[start : start + block]
            part_white = white[start : start + block]
            cov = jnp.einsum(
                "clm,jm->clj", xp, part_anom, precision=lax.Precision.HIGHEST
            ) / jnp.float32(MEMBERS - 1)
            total = total + jnp.einsum(
                "clj,jm->clm",
                cov * rho[:, None, start : start + block],
                part_white,
                precision=lax.Precision.HIGHEST,
            )
        prognostic_fields = (cube + total).reshape(tile_lat, tile_lon, LEV * MEMBERS)
    return prognostic_fields


def solution(mesh):
    placed = (
        P("lat", "lon", None),
        P("lat", "lon"),
        P("lat", "lon"),
        P("lat", "lon"),
        P(),
        P(),
        P(),
        P(),
        P(),
        P(),
        P(),
    )
    return jax.shard_map(
        body, mesh=mesh, in_specs=placed, out_specs=P("lat", "lon", None), check_vma=False
    )
```

profile of v0, /device:TPU:1, one launch (start us, length us, event | category | flops | bytes accessed | tf_op | source)
XLA Modules:
  0.0 1300.7 jit_solution(4321356358137888261)
XLA Ops:
  7.6 8.8 collective-permute-start.3
  30.8 8.1 collective-permute-start.7
  53.3 275.6 %all-reduce.5.cloned.1.call-done = f32[512,64]{0,1:T(8,128)} async-done(((f32[512,64]{0,1:T(8,128)}), f32[512,64]{0,1:T(8,128)}) %all-reduce.5.cloned.1.call-update) | async-done | bytes 131088 | tf_op jit(solution)/shard_map/psum | solution.py:112
  333.5 11.7 cholesky.374
  345.4 9.8 custom-call.33
  355.9 11.7 cholesky.393
  367.6 10.0 custom-call.34
  378.2 11.7 cholesky.414
  390.0 9.8 custom-call.35
  400.4 11.9 cholesky.431
  417.1 8.5 while.6
  426.1 39.3 %custom-call.36 = f32[4,128,128]{1,2,0:T(8,128)S(1)} custom-call(f32[4,128,128]{2,1,0:T(8,128)S(1)} %get-tuple-element.28), custom_call_target="InvertDiagBlocksLowerTriangular" | custom-call | tf_op jit(solution)/shard_map/jit(_cho_solve)/triangular_solve | solution.py:70
  477.2 258.3 %all-reduce.7.cloned.1.call-done = f32[512,64]{0,1:T(8,128)} async-done(((f32[512,64]{0,1:T(8,128)}), f32[512,64]{0,1:T(8,128)}) %all-reduce.7.cloned.1.call-update) | async-done | bytes 131088 | tf_op jit(solution)/shard_map/psum | solution.py:112
  740.5 11.7 cholesky.446
  752.9 9.8 custom-call.37
  763.4 11.7 cholesky.465
  775.6 9.9 custom-call.38
  786.2 11.7 cholesky.486
  798.6 9.8 custom-call.39
  809.0 11.9 cholesky.503
  828.7 7.7 while.7
  836.4 39.3 %custom-call.40 = f32[4,128,128]{1,2,0:T(8,128)S(1)} custom-call(f32[4,128,128]{2,1,0:T(8,128)S(1)} %get-tuple-element.29), custom_call_target="InvertDiagBlocksLowerTriangular" | custom-call | tf_op jit(solution)/shard_map/jit(_cho_solve)/triangular_solve | solution.py:70
  888.6 258.7 %all-reduce.9.cloned.1.call-done = f32[512,64]{0,1:T(8,128)} async-done(((f32[512,64]{0,1:T(8,128)}), f32[512,64]{0,1:T(8,128)}) %all-reduce.9.cloned.1.call-update) | async-done | bytes 131088 | tf_op jit(solution)/shard_map/psum | solution.py:112
  1152.2 11.7 cholesky.518
  1164.1 9.8 custom-call.41
  1174.6 11.7 cholesky.537
  1186.3 10.0 custom-call.42
  1197.0 11.7 cholesky.558
  1208.7 9.8 custom-call.43
  1219.1 11.9 cholesky.575
  1237.1 7.7 while.8
  1244.8 39.3 %custom-call.44 = f32[4,128,128]{1,2,0:T(8,128)S(1)} custom-call(f32[4,128,128]{2,1,0:T(8,128)S(1)} %get-tuple-element.30), custom_call_target="InvertDiagBlocksLowerTriangular" | custom-call | tf_op jit(solution)/shard_map/jit(_cho_solve)/triangular_solve | solution.py:70
  (358 shorter events, 120.6 us)
Async XLA Ops:
  6.5 322.4 %all-reduce.5.cloned.1.call-start = ((), (), s32[]{:S(2)}) async-start(), calls=%async_computation | async-start | bytes 262144 | tf_op jit(solution)/shard_map/psum | solution.py:112
  7.6 22.8 %collective-permute-start.3 = (f32[4,1,1792]{2,1,0:T(1,128)S(1)}, f32[4,1,1792]{2,1,0:T(1,128)S(1)}, u32[]{:S(2)}, u32[]{:S(2)}) collective-permute-start(f32[4,1,1792]{2,1,0:T(1,128)S(1)} %get-tuple-element.80), channel_id=1, source_target_pairs={{0,1},{1,2},{2,3},{3,4},{4,5},{5,6},{6,7},{7,8},{8,9},{9,10},{10,1... | collective-permute-start | bytes 86024 | tf_op jit(solution)/shard_map/ppermute | solution.py:22
  16.5 13.9 %collective-permute-start.2 = (f32[4,1,1792]{2,1,0:T(1,128)S(1)}, f32[4,1,1792]{2,1,0:T(1,128)S(1)}, u32[]{:S(2)}, u32[]{:S(2)}) collective-permute-start(f32[4,1,1792]{2,1,0:T(1,128)S(1)} %get-tuple-element.79), channel_id=1, source_target_pairs={{1,0},{2,1},{3,2},{4,3},{5,4},{6,5},{7,6},{8,7},{9,8},{10,9},{11,1... | collective-permute-start | bytes 86024 | tf_op jit(solution)/shard_map/ppermute | solution.py:25
  18.4 6.2 copy-start.22
  18.4 6.2 copy-start.38
  19.3 11.1 collective-permute-start
  20.6 9.8 collective-permute-start.1
  24.7 1.1 copy-start.35
  27.1 3.3 copy-start.6
  27.8 21.0 %copy-start.25 = (f32[1,512]{1,0:T(1,128)}, f32[1,512]{1,0:T(1,128)S(1)}, u32[]{:S(2)}) copy-start(f32[1,512]{1,0:T(1,128)S(1)} %get-tuple-element.138) | copy-start | bytes 6148
  27.8 21.6 %copy-start.23 = (f32[1,512]{1,0:T(1,128)}, f32[1,512]{1,0:T(1,128)S(1)}, u32[]{:S(2)}) copy-start(f32[1,512]{1,0:T(1,128)S(1)} %get-tuple-element.136) | copy-start | bytes 6148
  30.8 19.2 %collective-permute-start.7 = (f32[4,1,1792]{2,1,0:T(1,128)S(1)}, f32[4,1,1792]{2,1,0:T(1,128)S(1)}, u32[]{:S(2)}, u32[]{:S(2)}) collective-permute-start(f32[4,1,1792]{2,1,0:T(1,128)S(1)} %get-tuple-element.76), channel_id=1, source_target_pairs={{0,1},{1,2},{2,3},{3,4},{4,5},{5,6},{6,7},{7,8},{8,9},{9,10},{10,1... | collective-permute-start | bytes 86024 | tf_op jit(solution)/shard_map/ppermute | solution.py:22
  38.9 11.1 collective-permute-start.6
  43.5 6.5 collective-permute-start.4
  44.8 5.2 collective-permute-start.5
  52.5 683.0 %all-reduce.7.cloned.1.call-start = ((), (), s32[]{:S(2)}) async-start(), calls=%async_computation.1 | async-start | bytes 262144 | tf_op jit(solution)/shard_map/psum | solution.py:112
  328.9 1.0 copy-start.7
  332.5 1.0 copy-start
  333.5 21.7 %copy-start.1 = (f32[512,512]{1,0:T(8,128)S(1)}, f32[512,512]{1,0:T(8,128)}, u32[]{:S(2)}) copy-start(f32[512,512]{1,0:T(8,128)} %copy-done) | copy-start | bytes 3145732
  474.7 1.2 copy-start.41
  474.7 1.2 copy-start.42
  475.9 260.6 %copy-start.10 = (f32[3,512,64]{1,2,0:T(8,128)S(1)}, f32[3,512,64]{1,2,0:T(8,128)}, u32[]{:S(2)}) copy-start(f32[3,512,64]{1,2,0:T(8,128)} %param.26) | copy-start | bytes 1179652
  476.6 670.6 %all-reduce.9.cloned.1.call-start = ((), (), s32[]{:S(2)}) async-start(), calls=%async_computation.2 | async-start | bytes 262144 | tf_op jit(solution)/shard_map/psum | solution.py:112
  735.5 1.0 copy-start.8
  739.5 1.0 copy-start.2
  740.5 22.2 %copy-start.3 = (f32[512,512]{1,0:T(8,128)S(1)}, f32[512,512]{1,0:T(8,128)}, u32[]{:S(2)}) copy-start(f32[512,512]{1,0:T(8,128)} %copy-done.2) | copy-start | bytes 3145732
  878.9 0.7 copy-start.21
  880.3 0.7 copy-start.19
  1147.2 1.0 copy-start.9
  1151.2 1.0 copy-start.4
  1152.2 21.7 %copy-start.5 = (f32[512,512]{1,0:T(8,128)S(1)}, f32[512,512]{1,0:T(8,128)}, u32[]{:S(2)}) copy-start(f32[512,512]{1,0:T(8,128)} %copy-done.4) | copy-start | bytes 3145732
  1287.2 0.7 copy-start.17
  (26 other events, 17.6 us)
Sparse Core Ops, SparseCore 0:
  52.6 276.2 all-reduce.4
  476.8 258.6 all-reduce.6
  888.6 258.6 all-reduce.8
where the time goes:
time: 1300 us
  waiting for transfers between devices  793 us (61%)
  other arithmetic  369 us (28%)
  local copies, waits for them, and re-layouts  48.5 us (4%)
  starting transfers between devices  35 us (3%)
  matrix products  32.8 us (3%)
  between operations  22.6 us (2%)
    psum x3, waiting for transfers between devices, body(): lax.psum(jnp.where(mine[:, None], picked, jnp.float32(0.0)), ('lat', 'lon'))  793 us
    another operation x44, other arithmetic, whiten(): factor = jnp.linalg.cholesky(cov)  239 us
    another operation x7, other arithmetic, whiten(): return (anom, jax.scipy.linalg.cho_solve((factor, True), rhs))  118 us
  transfers between devices with their start and end apart: 11, of which 3 were waited for; matrix products, arithmetic and copies ran while one was open for 1% of the time, Pallas kernels for 0%

commit v1 on v0

v1 whole, which is shorter than its diff:
```python
import functools

import jax
import jax.numpy as jnp
from jax import lax
from jax.experimental import pallas as pl
from jax.experimental.pallas import tpu as pltpu
from jax.sharding import Mesh
from jax.sharding import PartitionSpec as P

LEV = 28
MEMBERS = 64
BATCH_GROUPS = 3
CAP = 4
NB = 512
CLAT = 4
CLON = 8
CELLS = CLAT * CLON
NLON = 256
N_LON = 32
WIDTH = LEV * MEMBERS
PACKED = WIDTH + 128
SLOTS = BATCH_GROUPS * CAP
ROWS = CELLS * LEV
OBS = BATCH_GROUPS * NB
HIGHEST = lax.Precision.HIGHEST
ADVECT = 0.2

LAT = ("x", "yl")
LON = ("z", "yh", "c")
PLANE = ("yl", "z", "yh")


def taper(dist, radius):
    z = dist / radius
    inner = 1.0 - 5.0 / 3.0 * z**2 + 0.625 * z**3 + 0.5 * z**4 - 0.25 * z**5
    outside = jnp.maximum(z, 1.0)
    outer = (
        4.0
        - 5.0 * outside
        + 5.0 / 3.0 * outside**2
        + 0.625 * outside**3
        - 0.5 * outside**4
        + outside**5 / 12.0
        - 2.0 / (3.0 * outside)
    )
    return jnp.where(z <= 1.0, inner, jnp.where(z < 2.0, outer, jnp.float32(0.0)))


def rho_of(lat_a, lon_a, lat_b, lon_b, radius_b):
    dlat = jnp.abs(lat_a[:, None] - lat_b[None, :]).astype(jnp.float32)
    dlon = jnp.abs(lon_a[:, None] - lon_b[None, :])
    dlon = jnp.minimum(dlon, NLON - dlon).astype(jnp.float32)
    dist = jnp.sqrt(dlat * dlat + dlon * dlon)
    return taper(dist, radius_b[None, :])


def forecast_kernel(site_ref, mid, lo, hi, west, east, x_ref, send_ref, grid, coef):
    grid[0:2, 0:8] = lo[...]
    grid[2:6, 0:8] = mid[...]
    grid[6:8, 0:8] = hi[...]
    grid[:, 8:16] = jnp.zeros((8, 8, PACKED), jnp.float32)
    grid[:, 8:10] = east[...]
    grid[:, 14:16] = west[...]
    winds = grid[1:7, :, WIDTH:PACKED]
    for n in range(3):
        coef[n] = jnp.broadcast_to(winds[:, :, n : n + 1], (6, 16, 128))

    def step(v, nw, ew, ss):
        here, north, south = v[1:-1], v[2:], v[:-2]
        east_of = pltpu.roll(here, 15, 1)
        west_of = pltpu.roll(here, 1, 1)
        lap = north + south + east_of + west_of - 4.0 * here
        return here + ss * lap - ADVECT * (nw * (north - south) + ew * (east_of - west_of))

    for chunk in range(WIDTH // 128):
        lanes = slice(chunk * 128, chunk * 128 + 128)
        first = step(grid[:, :, lanes], coef[0], coef[1], coef[2])
        second = step(first, coef[0, 1:5], coef[1, 1:5], coef[2, 1:5])
        x_ref[chunk] = second[:, 0:8].reshape(CELLS, 128)

    lane = lax.broadcasted_iota(jnp.int32, (1, 128), 1)
    for pair in range(SLOTS // 2):
        halves = []
        for half in range(2):
            site = site_ref[2 * pair + half]
            cell = site // LEV
            level = site - cell * LEV
            row = x_ref[level // 2, pl.ds(cell, 1), :]
            swap = (level % 2) != half
            halves.append(jnp.where(swap, pltpu.roll(row, 64, 1), row))
        both = jnp.where(lane < 64, halves[0], halves[1])
        send_ref[:, pair, :] = jnp.broadcast_to(both, (send_ref.shape[0], 128))
    send_ref[:, SLOTS // 2 :, :] = jnp.zeros((send_ref.shape[0], 2, 128), jnp.float32)


def forecast(sites, mid, lo, hi, west, east):
    vmem = pl.BlockSpec(memory_space=pltpu.VMEM)
    return pl.pallas_call(
        forecast_kernel,
        out_shape=(
            jax.ShapeDtypeStruct((WIDTH // 128, CELLS, 128), jnp.float32),
            jax.ShapeDtypeStruct((64, 8, 128), jnp.float32),
        ),
        in_specs=[pl.BlockSpec(memory_space=pltpu.SMEM)] + [vmem] * 5,
        out_specs=(vmem, vmem),
        scratch_shapes=[
            pltpu.VMEM((8, 16, PACKED), jnp.float32),
            pltpu.VMEM((3, 6, 16, 128), jnp.float32),
        ],
        compiler_params=pltpu.CompilerParams(vmem_limit_bytes=8 << 20),
        name="forecast",
    )(sites, mid, lo, hi, west, east)


def nt_dot(a, b):
    return lax.dot_general(
        a, b, (((1,), (1,)), ((), ())), precision=HIGHEST, preferred_element_type=jnp.float32
    )


def nn_dot(a, b):
    return lax.dot_general(
        a, b, (((1,), (0,)), ((), ())), precision=HIGHEST, preferred_element_type=jnp.float32
    )


def assimilate_kernel(
    row_ref, x_ref, mine, theirs, odd_ref, target_ref, rinv_ref, rho_obs, rho_own, out_ref, state, obs, every, rows_of
):
    every[0 : mine.shape[0], :] = mine[...]
    every[mine.shape[0] :, :] = theirs[...]

    @pl.loop(0, OBS // 16)
    def _(n):
        base = pl.multiple_of(n * 16, 16)
        for i in range(16):
            rows_of[pl.ds(base + i, 1), :] = every[pl.ds(row_ref[base + i], 1), :]

    picked = rows_of[...]
    obs[...] = jnp.where(odd_ref[...] > 0.5, picked[:, MEMBERS:], picked[:, :MEMBERS])
    for level in range(LEV):
        half = level % 2 * 64
        state[level * CELLS : (level + 1) * CELLS, :] = x_ref[level // 2, :, half : half + 64]
    row_id = lax.broadcasted_iota(jnp.int32, (MEMBERS, 1), 0)
    diag = lax.broadcasted_iota(jnp.int32, (MEMBERS, 128), 0) == lax.broadcasted_iota(
        jnp.int32, (MEMBERS, 128), 1
    )

    @pl.loop(0, BATCH_GROUPS)
    def _(k):
        here = pl.ds(pl.multiple_of(k * NB, NB), NB)
        prior = obs[here, :]
        anom = prior - jnp.mean(prior, axis=1, keepdims=True)
        rinv = rinv_ref[here, :]
        innovation = target_ref[here, :] - prior
        scaled = jnp.concatenate([anom * rinv, innovation * rinv], axis=1)
        work = nn_dot(anom.T, scaled)
        work = jnp.where(diag, work + jnp.float32(MEMBERS - 1), work)
        for p in range(MEMBERS):
            pivot = work[p : p + 1, :]
            factor = work[:, p : p + 1] * (1.0 / work[p : p + 1, p : p + 1])
            factor = jnp.where(row_id == p, 0.0, factor)
            work = work - factor * pivot
        pivots = jnp.sum(jnp.where(diag, work, 0.0), axis=1, keepdims=True)
        weights = work[:, MEMBERS:] / pivots
        white = (innovation - nn_dot(anom, weights)) * rinv * jnp.float32(1.0 / (MEMBERS - 1))

        def increment(block, rho):
            dev = block - jnp.mean(block, axis=1, keepdims=True)
            return nn_dot(nt_dot(dev, anom) * rho, white)

        @pl.loop(0, ROWS // 128)
        def _(n):
            rows = pl.ds(pl.multiple_of(n * 128, 128), 128)
            block = state[rows, :]
            rho = rho_own[k]
            state[rows, :] = block + increment(block, jnp.concatenate([rho] * 4, axis=0))

        @pl.loop((k + 1) * 4, BATCH_GROUPS * 4)
        def _(n):
            rows = pl.ds(pl.multiple_of(n * 128, 128), 128)
            from_rho = pl.ds(pl.multiple_of((n - 4 + 4 * k) * 128, 128), 128)
            block = obs[rows, :]
            obs[rows, :] = block + increment(block, rho_obs[from_rho, :])

    for level in range(0, LEV, 2):
        out_ref[:, level * 64 : level * 64 + 128] = jnp.concatenate(
            [state[level * CELLS : (level + 1) * CELLS, :], state[(level + 1) * CELLS : (level + 2) * CELLS, :]],
            axis=1,
        )


def assimilate(row, x, mine, theirs, odd, target, rinv, rho_obs, rho_own):
    vmem = pl.BlockSpec(memory_space=pltpu.VMEM)
    return pl.pallas_call(
        assimilate_kernel,
        out_shape=jax.ShapeDtypeStruct((CELLS, WIDTH), jnp.float32),
        in_specs=[pl.BlockSpec(memory_space=pltpu.SMEM)] + [vmem] * 8,
        out_specs=vmem,
        scratch_shapes=[
            pltpu.VMEM((ROWS, MEMBERS), jnp.float32),
            pltpu.VMEM((OBS, MEMBERS), jnp.float32),
            pltpu.VMEM((2 * 256 * SLOTS // 2, 128), jnp.float32),
            pltpu.VMEM((OBS, 128), jnp.float32),
        ],
        compiler_params=pltpu.CompilerParams(vmem_limit_bytes=24 << 20),
        name="assimilate",
    )(row, x, mine, theirs, odd, target, rinv, rho_obs, rho_own)


def plan(lat_tile, lon_tile, owner, site, obs_class, cutoff_table):
    cell = site // LEV
    glat = owner // N_LON * CLAT + cell // CLON
    glon = owner % N_LON * CLON + cell % CLON
    classes = jnp.arange(cutoff_table.shape[0], dtype=jnp.int32)
    match = (obs_class[:, :, None] == classes).astype(jnp.int32)
    radius = jnp.sum(match * cutoff_table, axis=2).astype(jnp.float32)
    order = jnp.arange(NB, dtype=jnp.int32)
    same = (owner[:, :, None] == owner[:, None, :]) & (order[None, :] < order[:, None])
    rank = jnp.sum(same.astype(jnp.int32), axis=2)
    slot = jnp.arange(BATCH_GROUPS, dtype=jnp.int32)[:, None] * CAP + rank
    mine = owner == lat_tile * N_LON + lon_tile
    chosen = mine[:, None, :] & (rank[:, None, :] == jnp.arange(CAP, dtype=jnp.int32)[:, None])
    sites = jnp.sum(jnp.where(chosen, site[:, None, :], 0), axis=2).reshape(SLOTS)
    lat, lon = owner // N_LON, owner % N_LON
    x, yl = lat // 4, lat % 4
    z, yh, c = lon // 4, lon // 2 % 2, lon % 2
    other = jnp.where(c == lon_tile % 2, 0, 1)
    row = (((other * 4 + x) * 64 + (yl * 8 + z) * 2 + yh) * (SLOTS // 2) + slot // 2).reshape(OBS)
    odd = jnp.broadcast_to((slot % 2).astype(jnp.float32).reshape(OBS, 1), (OBS, MEMBERS))
    rho_obs = jnp.concatenate(
        [
            rho_of(glat[1:].reshape(-1), glon[1:].reshape(-1), glat[0], glon[0], radius[0]),
            rho_of(glat[2], glon[2], glat[1], glon[1], radius[1]),
        ]
    )
    local = jnp.arange(CELLS, dtype=jnp.int32)
    cell_lat = lat_tile * CLAT + local // CLON
    cell_lon = lon_tile * CLON + local % CLON
    rho_own = jnp.stack(
        [rho_of(cell_lat, cell_lon, glat[k], glon[k], radius[k]) for k in range(BATCH_GROUPS)]
    )
    return sites, row, odd, rho_obs, rho_own


def halo(block, axes, count, dim, periodic):
    forward = [(i, i + 1) for i in range(count - 1)]
    if periodic:
        forward.append((count - 1, 0))
    backward = [(b, a) for a, b in forward]
    extent = block.shape[dim]
    low = lax.ppermute(lax.slice_in_dim(block, extent - 2, None, axis=dim), axes, forward)
    high = lax.ppermute(lax.slice_in_dim(block, 0, 2, axis=dim), axes, backward)
    return low, high


def body(
    ensemble,
    northward_wind,
    eastward_wind,
    spreading_strength,
    owner,
    site,
    obs_class,
    cutoff_table,
    obs_value,
    obs_var,
    obs_noise,
):
    lat_tile = lax.axis_index("x") * 4 + lax.axis_index("yl")
    lon_tile = lax.axis_index("z") * 4 + lax.axis_index("yh") * 2 + lax.axis_index("c")
    winds = jnp.stack([northward_wind, eastward_wind, spreading_strength], axis=2)
    winds = jnp.pad(winds, ((0, 0), (0, 0), (0, 125)))
    mid = jnp.concatenate([ensemble, winds], axis=2)
    lo, hi = halo(mid, LAT, 16, 0, False)
    tall = jnp.concatenate([lo, mid, hi], axis=0)
    west, east = halo(tall, LON, 32, 1, True)
    sites, row, odd, rho_obs, rho_own = plan(
        lat_tile, lon_tile, owner, site, obs_class, cutoff_table
    )
    target = (obs_value[:, :, None] + jnp.sqrt(obs_var)[:, :, None] * obs_noise).reshape(OBS, MEMBERS)
    rinv = jnp.broadcast_to((1.0 / obs_var).reshape(OBS, 1), (OBS, MEMBERS))
    state, send = forecast(sites, mid, lo, hi, west, east)
    plane = lax.all_to_all(send, PLANE, 0, 0)
    plane = plane[:, : SLOTS // 2, :].reshape(64 * SLOTS // 2, 128)
    cube = lax.all_to_all(jnp.broadcast_to(plane, (4,) + plane.shape), "x", 0, 0)
    cube = cube.reshape(-1, 128)
    partner = lax.ppermute(cube, "c", [(0, 1), (1, 0)])
    out = assimilate(row, state, cube, partner, odd, target, rinv, rho_obs, rho_own)
    return out.reshape(CLAT, CLON, WIDTH)


def solution(mesh):
    split = Mesh(mesh.devices.reshape(4, 4, 8, 2, 2), LAT + LON)
    tile = P(LAT, LON)
    return jax.shard_map(
        body,
        mesh=split,
        in_specs=(P(LAT, LON, None), tile, tile, tile) + (P(),) * 7,
        out_specs=P(LAT, LON, None),
        check_vma=False,
    )
```

time: 1300 us -> 137 us (0.11)
  waiting for transfers between devices: 793 us -> 26.8 us
  other arithmetic: 369 us -> 18.8 us
  Pallas kernels: 0 us -> 49.6 us
  local copies, waits for them, and re-layouts: 48.5 us -> 2.01 us
  matrix products: 32.8 us -> 0 us
  between operations: 22.6 us -> 0.28 us
    psum x3 -> x0, waiting for transfers between devices: 793 us -> none  [body(): lax.psum(jnp.where(mine[:, None], picked, jnp.float32(0.0)), ('lat', 'lon'))]
    another operation x51 -> x2, other arithmetic: 357 us -> 0.74 us  [the longest x1 0.72 us: body(): jnp.stack([northward_wind, eastward_wind, spreading_strength], axis=2)]
    pallas_call x0 -> x2, Pallas kernels: none -> 49.6 us  [the longest x1 47.6 us: assimilate(): pl.pallas_call(assimilate_kernel, out_shape=jax.ShapeDtypeStruct((CELLS,...]
    another operation x54 -> x1, local copies, waits for them, and re-layouts: 24.2 us -> 0.1 us  [body(): jnp.stack([northward_wind, eastward_wind, spreading_strength], axis=2)]
    all_to_all x0 -> x2, starting transfers between devices: none -> 20.7 us  [the longest x1 15 us: body(): plane = lax.all_to_all(send, PLANE, 0, 0)]
    all_to_all x0 -> x2, waiting for transfers between devices: none -> 18.1 us  [the longest x1 10.7 us: body(): lax.all_to_all(jnp.broadcast_to(plane, (4,) + plane.shape), 'x', 0, 0)]
    dot_general x27 -> x0, matrix products: 17.3 us -> none  [the longest x12 7.66 us: body(): jnp.einsum('clm,jm->clj', xp, part_anom, precision=lax.Precision.HIGHEST)]
    ppermute x8 -> x5, starting transfers between devices: 34 us -> 18.3 us  [the longest x2 13 us: halo(): lax.ppermute(lax.slice_in_dim(block, extent - 2, None, axis=dim), axes, f...]
  transfers between devices with their start and end apart: 11 -> 7, of which waited for: 3 -> 4; matrix products, arithmetic and copies ran while one was open for 1% -> 12% of each run, Pallas kernels for 0% -> 0%
where the time goes in v1:
time: 137 us; the launch traced here: 136 us
  Pallas kernels  49.6 us (36%)
  starting transfers between devices  38.9 us (28%)
  waiting for transfers between devices  26.8 us (20%)
  other arithmetic  18.8 us (14%)
  local copies, waits for them, and re-layouts  2.01 us (1%)
    pallas_call x1, Pallas kernels, assimilate(): pl.pallas_call(assimilate_kernel, out_shape=jax.ShapeDtypeStruct((CELLS,...  47.6 us
    all_to_all x1, starting transfers between devices, body(): plane = lax.all_to_all(send, PLANE, 0, 0)  15 us
    ppermute x2, starting transfers between devices, halo(): lax.ppermute(lax.slice_in_dim(block, extent - 2, None, axis=dim), axes, f...  13 us
    all_to_all x1, waiting for transfers between devices, body(): lax.all_to_all(jnp.broadcast_to(plane, (4,) + plane.shape), 'x', 0, 0)  10.7 us
    ppermute x2, waiting for transfers between devices, halo(): high = lax.ppermute(lax.slice_in_dim(block, 0, 2, axis=dim), axes, backward)  8.65 us
    select_n x3, other arithmetic, taper(): jnp.where(z <= 1.0, inner, jnp.where(z < 2.0, outer, jnp.float32(0.0)))  8.09 us
    all_to_all x1, waiting for transfers between devices, body(): plane = lax.all_to_all(send, PLANE, 0, 0)  7.46 us
    all_to_all x1, starting transfers between devices, body(): lax.all_to_all(jnp.broadcast_to(plane, (4,) + plane.shape), 'x', 0, 0)  5.7 us
  transfers between devices with their start and end apart: 7, of which 4 were waited for; matrix products, arithmetic and copies ran while one was open for 12% of the time, Pallas kernels for 0%

profile of v1, /device:TPU:1, one launch (start us, length us, event | category | flops | bytes accessed | tf_op | source)
XLA Modules:
  0.0 136.4 jit_solution(13732859115690855483)
XLA Ops:
  0.0 0.7 pad_maximum_fusion.7
  0.7 0.1 copy.22
  0.8 1.0 fusion.53
  1.8 4.0 %collective-permute-start = (f32[2,8,1920]{2,1,0:T(8,128)S(1)}, f32[2,8,1920]{2,1,0:T(8,128)S(1)}, u32[]{:S(2)}, u32[]{:S(2)}) collective-permute-start(f32[2,8,1920]{2,1,0:T(8,128)S(1)} %get-tuple-element.14), channel_id=1, source_target_pairs={{0,32},{32,64},{64,96},{96,128},{128,160},{160,192},{192,224},{224... | collective-permute-start | bytes 368648 | tf_op jit(solution)/shard_map/ppermute | solution.py:253
  5.8 1.3 collective-permute-start.1
  7.2 1.0 pad_maximum_fusion.1.mid
  8.2 0.8 select_reduce_fusion
  9.0 1.6 %convert_reduce_fusion = s32[3,512]{1,0:T(4,128)S(1)} fusion(s32[3,512]{1,0:T(4,128)} %param.15, pred[512,512]{1,0:T(8,128)(4,1)S(1)} %iota_compare_fusion), kind=kLoop, calls=%fused_computation.2 | loop fusion | flops 3144192 | bytes 274432 | tf_op jit(solution)/shard_map/reduce_sum | solution.py:221
  10.7 0.8 fusion.148
  11.5 0.7 broadcast_compare_fusion
  12.3 0.9 select_reduce_fusion.1
  13.1 0.1 reshape.853.site_ref
  13.2 0.4 collective-permute-done.1.hi
  13.6 1.1 pad_maximum_fusion.3
  14.7 8.9 %collective-permute-start.2 = (f32[8,2,1920]{2,1,0:T(2,128)S(1)}, f32[8,2,1920]{2,1,0:T(2,128)S(1)}, u32[]{:S(2)}, u32[]{:S(2)}) collective-permute-start(f32[8,2,1920]{2,1,0:T(2,128)S(1)} %get-tuple-element.12), channel_id=1, source_target_pairs={{0,1},{1,2},{2,3},{3,4},{4,5},{5,6},{6,7},{7,8},{8,9},{9,10},{10,1... | collective-permute-start | bytes 368648 | tf_op jit(solution)/shard_map/ppermute | solution.py:253
  23.7 1.9 %collective-permute-start.3 = (f32[8,2,1920]{2,1,0:T(2,128)S(1)}, f32[8,2,1920]{2,1,0:T(2,128)S(1)}, u32[]{:S(2)}, u32[]{:S(2)}) collective-permute-start(f32[8,2,1920]{2,1,0:T(2,128)S(1)} %get-tuple-element.11), channel_id=1, source_target_pairs={{1,0},{2,1},{3,2},{4,3},{5,4},{6,5},{7,6},{8,7},{9,8},{10,9},{11,1... | collective-permute-start | bytes 368648 | tf_op jit(solution)/shard_map/ppermute | solution.py:254
  25.6 8.3 %collective-permute-done.3.east = f32[8,2,1920]{2,1,0:T(2,128)S(1)} collective-permute-done((f32[8,2,1920]{2,1,0:T(2,128)S(1)}, f32[8,2,1920]{2,1,0:T(2,128)S(1)}, u32[]{:S(2)}, u32[]{:S(2)}) %collective-permute-start.3) | collective-permute-done | bytes 122912 | tf_op jit(solution)/shard_map/ppermute | solution.py:254
  33.9 2.0 %forecast.1 = (f32[14,32,128]{2,1,0:T(8,128)S(1)}, f32[64,8,128]{2,1,0:T(8,128)}) custom-call(s32[12]{0:T(128)S(1)} %reshape.853.site_ref, f32[4,8,1920]{2,1,0:T(8,128)S(1)} %pad_maximum_fusion.1.mid, f32[2,8,1920]{2,1,0:T(8,128)S(1)} %collective-permute-done.lo, f32[2,8,1920]{2,1,0:T(8,128)S(1)} %collective-permute-done.1.hi, ...), custom_call_target="tpu_custom_call" | custom-call | tf_op jit(solution)/shard_map/forecast/pallas_call | solution.py:99
  36.0 15.0 %all-to-all-start = ((f32[64,8,128]{2,1,0:T(8,128)}), f32[64,8,128]{2,1,0:T(8,128)S(1)}, u32[]{:S(2)}, u32[]{:S(2)}) async-start(f32[64,8,128]{2,1,0:T(8,128)} %get-tuple-element.8), calls=%async_computation | async-start | bytes 524288 | tf_op jit(solution)/shard_map/all_to_all | solution.py:285
  51.0 5.6 %fusion.6 = f32[1024,512]{1,0:T(8,128)} fusion(f32[512]{0:T(512)S(1)} %bitcast.40, s32[512]{0:T(512)S(1)} %bitcast.36, s32[1024]{0:T(1024)S(1)} %bitcast.43, s32[512]{0:T(512)S(1)} %bitcast.34, s32[1024]{0:T(1024)S(1)} %bitcast.42), kind=kLoop, calls=%fused_computation.15 | loop fusion | flops 24117248 | bytes 2111488 | tf_op jit(solution)/shard_map/jit(_where)/select_n | solution.py:47
  56.6 7.5 %all-to-all-done = f32[64,8,128]{2,1,0:T(8,128)S(1)} async-done(((f32[64,8,128]{2,1,0:T(8,128)}), f32[64,8,128]{2,1,0:T(8,128)S(1)}, u32[]{:S(2)}, u32[]{:S(2)}) %all-to-all-start) | async-done | bytes 262176 | tf_op jit(solution)/shard_map/all_to_all | solution.py:285
  64.1 0.9 broadcast_in_dim.40
  65.0 5.7 %all-to-all-start.1 = ((f32[4,384,128]{2,1,0:T(8,128)}), f32[4,384,128]{2,1,0:T(8,128)S(1)}, u32[]{:S(2)}, u32[]{:S(2)}) async-start(f32[4,384,128]{2,1,0:T(8,128)} %broadcast_in_dim.40), calls=%async_computation.1 | async-start | bytes 1572864 | tf_op jit(solution)/shard_map/all_to_all | solution.py:287
  70.8 0.3 copy.23
  71.0 0.5 fusion.68
  71.5 10.7 %all-to-all-done.1 = f32[4,384,128]{2,1,0:T(8,128)S(1)} async-done(((f32[4,384,128]{2,1,0:T(8,128)}), f32[4,384,128]{2,1,0:T(8,128)S(1)}, u32[]{:S(2)}, u32[]{:S(2)}) %all-to-all-start.1) | async-done | bytes 786464 | tf_op jit(solution)/shard_map/all_to_all | solution.py:287
  82.2 2.1 %collective-permute-start.4 = (f32[1536,128]{1,0:T(8,128)S(1)}, f32[1536,128]{1,0:T(8,128)S(1)}, u32[]{:S(2)}, u32[]{:S(2)}) collective-permute-start(f32[1536,128]{1,0:T(8,128)S(1)} %bitcast.22), channel_id=1, source_target_pairs={{0,1},{1,0},{2,3},{3,2},{4,5},{5,4},{6,7},{7,6},{8,9},{9,8},{10,11... | collective-permute-start | bytes 2359304 | tf_op jit(solution)/shard_map/ppermute | solution.py:289
  84.3 2.1 %fusion.32 = f32[512,512]{1,0:T(8,128)S(1)} fusion(f32[512]{0:T(512)S(1)} %bitcast.39, s32[512]{0:T(512)S(1)} %bitcast.33, s32[512]{0:T(512)S(1)} %bitcast.31, s32[512]{0:T(512)S(1)} %bitcast.27, s32[512]{0:T(512)S(1)} %bitcast.29), kind=kLoop, calls=%fused_computation.50 | loop fusion | flops 12058624 | bytes 1058816 | tf_op jit(solution)/shard_map/jit(_where)/select_n | solution.py:47
  86.4 1.9 %pad_maximum_fusion.rho_obs = f32[1536,512]{1,0:T(8,128)S(1)} fusion(f32[512,512]{1,0:T(8,128)S(1)} %fusion.32, f32[1024,512]{1,0:T(8,128)} %fusion.6), kind=kLoop, calls=%fused_computation | loop fusion | flops 786432 | bytes 6291456 | tf_op jit(solution)/shard_map/concatenate | solution.py:232
  88.3 0.3 broadcast_in_dim.41.odd_ref
  88.6 0.3 broadcast_in_dim.43.rinv_ref
  88.8 47.6 %assimilate.1 = f32[32,1792]{1,0:T(8,128)} custom-call(s32[1536]{0:T(1024)S(1)} %reshape.852.row_ref, f32[14,32,128]{2,1,0:T(8,128)S(1)} %get-tuple-element.7.x_ref, f32[1536,128]{1,0:T(8,128)S(1)} %bitcast.23, f32[1536,128]{1,0:T(8,128)S(1)} %collective-permute-done.4.theirs, f32[1536,64]{1,0:T(8,128)S(1)} %broadcast_in_dim.41.odd_ref, ...), custom_call_target="tpu_custom_call" | custom-call | tf_op jit(solution)/shard_map/assimilate/pallas_call | solution.py:196
  (27 shorter events, 0.3 us)
Async XLA Ops:
  1.8 11.4 %collective-permute-start = (f32[2,8,1920]{2,1,0:T(8,128)S(1)}, f32[2,8,1920]{2,1,0:T(8,128)S(1)}, u32[]{:S(2)}, u32[]{:S(2)}) collective-permute-start(f32[2,8,1920]{2,1,0:T(8,128)S(1)} %get-tuple-element.14), channel_id=1, source_target_pairs={{0,32},{32,64},{64,96},{96,128},{128,160},{160,192},{192,224},{224... | collective-permute-start | bytes 368648 | tf_op jit(solution)/shard_map/ppermute | solution.py:253
  5.8 7.8 %collective-permute-start.1 = (f32[2,8,1920]{2,1,0:T(8,128)S(1)}, f32[2,8,1920]{2,1,0:T(8,128)S(1)}, u32[]{:S(2)}, u32[]{:S(2)}) collective-permute-start(f32[2,8,1920]{2,1,0:T(8,128)S(1)} %get-tuple-element.13), channel_id=1, source_target_pairs={{32,0},{64,32},{96,64},{128,96},{160,128},{192,160},{224,192},{256... | collective-permute-start | bytes 368648 | tf_op jit(solution)/shard_map/ppermute | solution.py:254
  12.3 44.3 %copy-start.2 = (f32[3,512]{1,0:T(4,128)S(1)}, f32[3,512]{1,0:T(4,128)}, u32[]{:S(2)}) copy-start(f32[3,512]{1,0:T(4,128)} %param.20) | copy-start | bytes 18436
  13.2 43.3 %copy-start = (f32[3,512,64]{1,2,0:T(8,128)S(1)}, f32[3,512,64]{1,2,0:T(8,128)}, u32[]{:S(2)}) copy-start(f32[3,512,64]{1,2,0:T(8,128)} %param.21) | copy-start | bytes 1179652
  13.2 43.4 %copy-start.1 = (f32[3,512]{1,0:T(4,128)S(1)}, f32[3,512]{1,0:T(4,128)}, u32[]{:S(2)}) copy-start(f32[3,512]{1,0:T(4,128)} %param.19) | copy-start | bytes 18436
  14.7 10.9 %collective-permute-start.2 = (f32[8,2,1920]{2,1,0:T(2,128)S(1)}, f32[8,2,1920]{2,1,0:T(2,128)S(1)}, u32[]{:S(2)}, u32[]{:S(2)}) collective-permute-start(f32[8,2,1920]{2,1,0:T(2,128)S(1)} %get-tuple-element.12), channel_id=1, source_target_pairs={{0,1},{1,2},{2,3},{3,4},{4,5},{5,6},{6,7},{7,8},{8,9},{9,10},{10,1... | collective-permute-start | bytes 368648 | tf_op jit(solution)/shard_map/ppermute | solution.py:253
  23.7 10.2 %collective-permute-start.3 = (f32[8,2,1920]{2,1,0:T(2,128)S(1)}, f32[8,2,1920]{2,1,0:T(2,128)S(1)}, u32[]{:S(2)}, u32[]{:S(2)}) collective-permute-start(f32[8,2,1920]{2,1,0:T(2,128)S(1)} %get-tuple-element.11), channel_id=1, source_target_pairs={{1,0},{2,1},{3,2},{4,3},{5,4},{6,5},{7,6},{8,7},{9,8},{10,9},{11,1... | collective-permute-start | bytes 368648 | tf_op jit(solution)/shard_map/ppermute | solution.py:254
  36.0 28.1 %all-to-all-start = ((f32[64,8,128]{2,1,0:T(8,128)}), f32[64,8,128]{2,1,0:T(8,128)S(1)}, u32[]{:S(2)}, u32[]{:S(2)}) async-start(f32[64,8,128]{2,1,0:T(8,128)} %get-tuple-element.8), calls=%async_computation | async-start | bytes 524288 | tf_op jit(solution)/shard_map/all_to_all | solution.py:285
  65.0 17.2 %all-to-all-start.1 = ((f32[4,384,128]{2,1,0:T(8,128)}), f32[4,384,128]{2,1,0:T(8,128)S(1)}, u32[]{:S(2)}, u32[]{:S(2)}) async-start(f32[4,384,128]{2,1,0:T(8,128)} %broadcast_in_dim.40), calls=%async_computation.1 | async-start | bytes 1572864 | tf_op jit(solution)/shard_map/all_to_all | solution.py:287
  82.2 6.1 %collective-permute-start.4 = (f32[1536,128]{1,0:T(8,128)S(1)}, f32[1536,128]{1,0:T(8,128)S(1)}, u32[]{:S(2)}, u32[]{:S(2)}) collective-permute-start(f32[1536,128]{1,0:T(8,128)S(1)} %bitcast.22), channel_id=1, source_target_pairs={{0,1},{1,0},{2,3},{3,2},{4,5},{5,4},{6,7},{7,6},{8,9},{9,8},{10,11... | collective-permute-start | bytes 2359304 | tf_op jit(solution)/shard_map/ppermute | solution.py:289

commit v2 on v1

v2 whole, which is shorter than its diff:
```python
import functools

import jax
import jax.numpy as jnp
from jax import lax
from jax.experimental import pallas as pl
from jax.experimental.pallas import tpu as pltpu
from jax.sharding import Mesh
from jax.sharding import PartitionSpec as P

LEV = 28
MEMBERS = 64
BATCH_GROUPS = 3
CAP = 4
NB = 512
CLAT = 4
CLON = 8
CELLS = CLAT * CLON
NLON = 256
N_LON = 32
WIDTH = LEV * MEMBERS
PACKED = WIDTH + 128
SLOTS = BATCH_GROUPS * CAP
ROWS = CELLS * LEV
OBS = BATCH_GROUPS * NB
HIGHEST = lax.Precision.HIGHEST
ADVECT = 0.2

LAT = ("x", "yl")
LON = ("z", "yh", "c")
PLANE = ("yl", "z", "yh")


def taper(dist, radius):
    z = dist / radius
    inner = 1.0 - 5.0 / 3.0 * z**2 + 0.625 * z**3 + 0.5 * z**4 - 0.25 * z**5
    outside = jnp.maximum(z, 1.0)
    outer = (
        4.0
        - 5.0 * outside
        + 5.0 / 3.0 * outside**2
        + 0.625 * outside**3
        - 0.5 * outside**4
        + outside**5 / 12.0
        - 2.0 / (3.0 * outside)
    )
    return jnp.where(z <= 1.0, inner, jnp.where(z < 2.0, outer, jnp.float32(0.0)))


def rho_of(lat_a, lon_a, lat_b, lon_b, radius_b):
    dlat = jnp.abs(lat_a[:, None] - lat_b[None, :]).astype(jnp.float32)
    dlon = jnp.abs(lon_a[:, None] - lon_b[None, :])
    dlon = jnp.minimum(dlon, NLON - dlon).astype(jnp.float32)
    dist = jnp.sqrt(dlat * dlat + dlon * dlon)
    return taper(dist, radius_b[None, :])


def forecast_kernel(site_ref, mid, lo, hi, from_core, from_chip, x_ref, send_ref, grid, coef):
    grid[0:2, 0:8] = lo[...]
    grid[2:6, 0:8] = mid[...]
    grid[6:8, 0:8] = hi[...]
    grid[:, 8:16] = jnp.zeros((8, 8, PACKED), jnp.float32)
    second = site_ref[SLOTS] == 1
    grid[:, 8:10] = jnp.where(second, from_chip[...], from_core[...])
    grid[:, 14:16] = jnp.where(second, from_core[...], from_chip[...])
    winds = grid[1:7, :, WIDTH:PACKED]
    for n in range(3):
        coef[n] = jnp.broadcast_to(winds[:, :, n : n + 1], (6, 16, 128))

    def step(v, nw, ew, ss):
        here, north, south = v[1:-1], v[2:], v[:-2]
        east_of = pltpu.roll(here, 15, 1)
        west_of = pltpu.roll(here, 1, 1)
        lap = north + south + east_of + west_of - 4.0 * here
        return here + ss * lap - ADVECT * (nw * (north - south) + ew * (east_of - west_of))

    for chunk in range(WIDTH // 128):
        lanes = slice(chunk * 128, chunk * 128 + 128)
        first = step(grid[:, :, lanes], coef[0], coef[1], coef[2])
        second = step(first, coef[0, 1:5], coef[1, 1:5], coef[2, 1:5])
        x_ref[chunk] = second[:, 0:8].reshape(CELLS, 128)

    lane = lax.broadcasted_iota(jnp.int32, (1, 128), 1)
    for pair in range(SLOTS // 2):
        halves = []
        for half in range(2):
            site = site_ref[2 * pair + half]
            cell = site // LEV
            level = site - cell * LEV
            row = x_ref[level // 2, pl.ds(cell, 1), :]
            swap = (level % 2) != half
            halves.append(jnp.where(swap, pltpu.roll(row, 64, 1), row))
        both = jnp.where(lane < 64, halves[0], halves[1])
        send_ref[:, pair, :] = jnp.broadcast_to(both, (send_ref.shape[0], 128))
    send_ref[:, SLOTS // 2 :, :] = jnp.zeros((send_ref.shape[0], 2, 128), jnp.float32)


def forecast(sites, mid, lo, hi, from_core, from_chip):
    vmem = pl.BlockSpec(memory_space=pltpu.VMEM)
    return pl.pallas_call(
        forecast_kernel,
        out_shape=(
            jax.ShapeDtypeStruct((WIDTH // 128, CELLS, 128), jnp.float32),
            pltpu.VMEM((64, 8, 128), jnp.float32),
        ),
        in_specs=[pl.BlockSpec(memory_space=pltpu.SMEM)] + [vmem] * 5,
        out_specs=(vmem, vmem),
        scratch_shapes=[
            pltpu.VMEM((8, 16, PACKED), jnp.float32),
            pltpu.VMEM((3, 6, 16, 128), jnp.float32),
        ],
        compiler_params=pltpu.CompilerParams(vmem_limit_bytes=8 << 20),
        name="forecast",
    )(sites, mid, lo, hi, from_core, from_chip)


def full_dot(a, b):
    return lax.dot_general(
        a, b, (((1,), (0,)), ((), ())), precision=HIGHEST, preferred_element_type=jnp.float32
    )


def high(v):
    return v.astype(jnp.bfloat16).astype(jnp.float32)


def assimilate_kernel(
    row_ref, x_ref, mine, theirs, odd_ref, target_ref, rinv_ref, rho_one, rho_two, rho_own,
    out_ref, state, obs, every, rows_of, anom_split, white_split,
):
    left = lax.broadcasted_iota(jnp.int32, (1, 128), 1) < MEMBERS
    every[0 : mine.shape[0], :] = mine[...]
    every[mine.shape[0] :, :] = theirs[...]

    @pl.loop(0, OBS // 16)
    def _(n):
        base = pl.multiple_of(n * 16, 16)
        for i in range(16):
            rows_of[pl.ds(base + i, 1), :] = every[pl.ds(row_ref[base + i], 1), :]

    for level in range(0, LEV, 2):
        both = x_ref[level // 2]
        swapped = pltpu.roll(both, MEMBERS, 1)
        state[level * CELLS : (level + 1) * CELLS, :] = jnp.where(left, both, swapped)
        state[(level + 1) * CELLS : (level + 2) * CELLS, :] = jnp.where(left, swapped, both)
    picked = rows_of[...]
    swapped = pltpu.roll(picked, MEMBERS, 1)
    odd = odd_ref[...] > 0.5
    first = jnp.where(odd, swapped, picked)
    obs[...] = jnp.where(left, first, jnp.where(odd, picked, swapped))

    row_id = lax.broadcasted_iota(jnp.int32, (MEMBERS, 128), 0)
    lane_id = lax.broadcasted_iota(jnp.int32, (MEMBERS, 128), 1)
    diag = row_id == lane_id

    def centred(v):
        return v - jnp.sum(v, axis=1, keepdims=True) * jnp.float32(1.0 / 128)

    @pl.loop(0, BATCH_GROUPS)
    def _(k):
        here = pl.ds(pl.multiple_of(k * NB, NB), NB)
        prior = obs[here, :]
        anom = centred(prior)
        rinv = rinv_ref[here, :]
        innovation = target_ref[here, :] - prior
        anom_high = high(anom)
        anom_split[:, 0:128] = anom_high.astype(jnp.bfloat16)
        anom_split[:, 128:256] = (anom - anom_high).astype(jnp.bfloat16)
        work = full_dot(anom.T[:MEMBERS], jnp.where(left, anom, innovation) * rinv)
        work = jnp.where(diag, work + jnp.float32(MEMBERS - 1), work)
        for p in range(0, MEMBERS, 4):
            cols = [jnp.broadcast_to(work[:, p + t : p + t + 1], (MEMBERS, 128)) for t in range(4)]
            rows = [work[p + t : p + t + 1, :] for t in range(4)]
            e = [[cols[t][p + r : p + r + 1] for t in range(4)] for r in range(4)]
            det = 1.0 / (e[0][0] * e[1][1] - e[0][1] * e[1][0])
            top = [(e[1][1] * rows[0] - e[0][1] * rows[1]) * det, (e[0][0] * rows[1] - e[1][0] * rows[0]) * det]
            u = [[(e[1][1] * e[0][t] - e[0][1] * e[1][t]) * det for t in (2, 3)],
                 [(e[0][0] * e[1][t] - e[1][0] * e[0][t]) * det for t in (2, 3)]]
            s2 = [[e[r][t] - e[r][0] * u[0][t - 2] - e[r][1] * u[1][t - 2] for t in (2, 3)] for r in (2, 3)]
            low = [rows[r] - e[r][0] * top[0] - e[r][1] * top[1] for r in (2, 3)]
            det2 = 1.0 / (s2[0][0] * s2[1][1] - s2[0][1] * s2[1][0])
            new2 = (s2[1][1] * low[0] - s2[0][1] * low[1]) * det2
            new3 = (s2[0][0] * low[1] - s2[1][0] * low[0]) * det2
            new0 = top[0] - u[0][0] * new2 - u[0][1] * new3
            new1 = top[1] - u[1][0] * new2 - u[1][1] * new3
            new = [new0, new1, new2, new3]
            fresh = work
            for t in range(4):
                fresh = fresh - cols[t] * new[t]
            for t in range(4):
                fresh = jnp.where(row_id == p + t, new[t], fresh)
            work = fresh
        weights = jnp.where(left, pltpu.roll(work, MEMBERS, 1), work)
        white = innovation - full_dot(anom[:, :MEMBERS], weights)
        white = white * rinv * jnp.float32(1.0 / (MEMBERS - 1))
        white_high = high(white)
        white_split[...] = jnp.where(left, white_high, white - white_high).astype(jnp.bfloat16)

        def updated(block, rho):
            dev = centred(block)
            dev_high = high(dev)
            dev = jnp.where(left, dev_high, dev - dev_high).astype(jnp.bfloat16)
            cov = lax.dot_general(
                jnp.concatenate([dev, dev], axis=1),
                anom_split[...],
                (((1,), (1,)), ((), ())),
                preferred_element_type=jnp.float32,
            )
            cov = cov.reshape((-1,) + rho.shape) * rho
            cov = cov.reshape(-1, NB)
            cov_high = cov.astype(jnp.bfloat16)
            cov_low = (cov - cov_high.astype(jnp.float32)).astype(jnp.bfloat16)
            total = jnp.dot(cov_high, white_split[...], preferred_element_type=jnp.float32)
            total += jnp.dot(cov_low, white_split[...], preferred_element_type=jnp.float32)
            return block + (total + pltpu.roll(total, MEMBERS, 1))

        step = ROWS // 2

        @pl.loop(0, ROWS // step)
        def _(n):
            rows = pl.ds(pl.multiple_of(n * step, step), step)
            state[rows, :] = updated(state[rows, :], rho_own[k])

        def replay(first, rho):
            @pl.loop(0, rho.shape[0] // NB)
            def _(n):
                rows = pl.ds(pl.multiple_of(first + n * NB, NB), NB)
                from_rho = pl.ds(pl.multiple_of(n * NB, NB), NB)
                obs[rows, :] = updated(obs[rows, :], rho[from_rho, :])

        pl.when(k == 0)(lambda: replay(NB, rho_one))
        pl.when(k == 1)(lambda: replay(2 * NB, rho_two))

    for level in range(0, LEV, 2):
        low = state[level * CELLS : (level + 1) * CELLS, :]
        upper = state[(level + 1) * CELLS : (level + 2) * CELLS, :]
        out_ref[:, level * MEMBERS : (level + 2) * MEMBERS] = jnp.where(left, low, upper)


def assimilate(row, x, mine, theirs, odd, target, rinv, rho_one, rho_two, rho_own):
    vmem = pl.BlockSpec(memory_space=pltpu.VMEM)
    return pl.pallas_call(
        assimilate_kernel,
        out_shape=jax.ShapeDtypeStruct((CELLS, WIDTH), jnp.float32),
        in_specs=[pl.BlockSpec(memory_space=pltpu.SMEM)] + [vmem] * 9,
        out_specs=vmem,
        scratch_shapes=[
            pltpu.VMEM((ROWS, 128), jnp.float32),
            pltpu.VMEM((OBS, 128), jnp.float32),
            pltpu.VMEM((2 * 256 * SLOTS // 2, 128), jnp.float32),
            pltpu.VMEM((OBS, 128), jnp.float32),
            pltpu.VMEM((NB, 256), jnp.bfloat16),
            pltpu.VMEM((NB, 128), jnp.bfloat16),
        ],
        compiler_params=pltpu.CompilerParams(vmem_limit_bytes=24 << 20),
        name="assimilate",
    )(row, x, mine, theirs, odd, target, rinv, rho_one, rho_two, rho_own)


def slots(lat_tile, lon_tile, owner, site):
    order = jnp.arange(NB, dtype=jnp.int32)
    same = (owner[:, :, None] == owner[:, None, :]) & (order[None, :] < order[:, None])
    rank = jnp.sum(same.astype(jnp.int32), axis=2)
    slot = jnp.arange(BATCH_GROUPS, dtype=jnp.int32)[:, None] * CAP + rank
    mine = owner == lat_tile * N_LON + lon_tile
    chosen = mine[:, None, :] & (rank[:, None, :] == jnp.arange(CAP, dtype=jnp.int32)[:, None])
    sites = jnp.sum(jnp.where(chosen, site[:, None, :], 0), axis=2).reshape(SLOTS)
    lat, lon = owner // N_LON, owner % N_LON
    x, yl = lat // 4, lat % 4
    z, yh, c = lon // 4, lon // 2 % 2, lon % 2
    other = jnp.where(c == lon_tile % 2, 0, 1)
    row = ((other * 4 + x) * 64 + (yl * 8 + z) * 2 + yh) * (SLOTS // 2) + slot // 2
    return jnp.append(sites, lon_tile % 2), row.reshape(OBS), slot % 2


def tapers(lat_tile, lon_tile, owner, site, obs_class, cutoff_table):
    cell = site // LEV
    glat = owner // N_LON * CLAT + cell // CLON
    glon = owner % N_LON * CLON + cell % CLON
    classes = jnp.arange(cutoff_table.shape[0], dtype=jnp.int32)
    match = (obs_class[:, :, None] == classes).astype(jnp.int32)
    radius = jnp.sum(match * cutoff_table, axis=2).astype(jnp.float32)
    rho_one = rho_of(glat[1:].reshape(-1), glon[1:].reshape(-1), glat[0], glon[0], radius[0])
    rho_two = rho_of(glat[2], glon[2], glat[1], glon[1], radius[1])
    local = jnp.arange(CELLS, dtype=jnp.int32)
    cell_lat = lat_tile * CLAT + local // CLON
    cell_lon = lon_tile * CLON + local % CLON
    rho_own = jnp.stack(
        [rho_of(cell_lat, cell_lon, glat[k], glon[k], radius[k]) for k in range(BATCH_GROUPS)]
    )
    return rho_one, rho_two, rho_own


def lat_halo(block):
    forward = [(i, i + 1) for i in range(15)]
    backward = [(b, a) for a, b in forward]
    low = lax.ppermute(block[CLAT - 2 :], LAT, forward)
    high = lax.ppermute(block[:2], LAT, backward)
    return low, high


def lon_halo(block):
    second = lax.axis_index("c") == 1
    start, end = block[:, :2], block[:, CLON - 2 :]
    inner = jnp.where(second, start, end)
    outer = jnp.where(second, end, start)
    from_core = lax.ppermute(inner, "c", [(0, 1), (1, 0)])
    pairs = [(i, (i + 1) % N_LON) for i in range(1, N_LON, 2)]
    from_chip = lax.ppermute(outer, LON, pairs + [(b, a) for a, b in pairs])
    return from_core, from_chip


def body(
    ensemble,
    northward_wind,
    eastward_wind,
    spreading_strength,
    owner,
    site,
    obs_class,
    cutoff_table,
    obs_value,
    obs_var,
    obs_noise,
):
    lat_tile = lax.axis_index("x") * 4 + lax.axis_index("yl")
    lon_tile = lax.axis_index("z") * 4 + lax.axis_index("yh") * 2 + lax.axis_index("c")
    winds = jnp.stack([northward_wind, eastward_wind, spreading_strength], axis=2)
    winds = jnp.pad(winds, ((0, 0), (0, 0), (0, 125)))
    mid = jnp.concatenate([ensemble, winds], axis=2)
    lo, hi = lat_halo(mid)
    tall = jnp.concatenate([lo, mid, hi], axis=0)
    from_core, from_chip = lon_halo(tall)
    sites, row, parity = slots(lat_tile, lon_tile, owner, site)
    state, send = forecast(sites, mid, lo, hi, from_core, from_chip)
    send, parity, owner, site, obs_class, obs_var, obs_value, obs_noise = lax.optimization_barrier(
        (send, parity, owner, site, obs_class, obs_var, obs_value, obs_noise)
    )
    rho_one, rho_two, rho_own = tapers(lat_tile, lon_tile, owner, site, obs_class, cutoff_table)
    odd = jnp.broadcast_to(parity.astype(jnp.float32).reshape(OBS, 1), (OBS, 128))
    target = (obs_value[:, :, None] + jnp.sqrt(obs_var)[:, :, None] * obs_noise).reshape(OBS, MEMBERS)
    target = jnp.concatenate([target, target], axis=1)
    rinv = jnp.broadcast_to((1.0 / obs_var).reshape(OBS, 1), (OBS, 128))
    plane = lax.all_to_all(send, PLANE, 0, 0)
    plane = plane[:, : SLOTS // 2, :].reshape(64 * SLOTS // 2, 128)
    cube = lax.all_gather(plane, "x", tiled=True)
    partner = lax.ppermute(cube, "c", [(0, 1), (1, 0)])
    out = assimilate(row, state, cube, partner, odd, target, rinv, rho_one, rho_two, rho_own)
    return out.reshape(CLAT, CLON, WIDTH)


def solution(mesh):
    split = Mesh(mesh.devices.reshape(4, 4, 8, 2, 2), LAT + LON)
    tile = P(LAT, LON)
    return jax.shard_map(
        body,
        mesh=split,
        in_specs=(P(LAT, LON, None), tile, tile, tile) + (P(),) * 7,
        out_specs=P(LAT, LON, None),
        check_vma=False,
    )
```

time: 137 us -> 109 us (0.80)
  Pallas kernels: 49.6 us -> 22.1 us
  blocking collectives: 0 us -> 13.7 us
  waiting for transfers between devices: 26.8 us -> 14.5 us
  other arithmetic: 18.8 us -> 15.9 us
  local copies, waits for them, and re-layouts: 2.01 us -> 3.7 us
    pallas_call x1, Pallas kernels: 47.6 us -> 20.1 us  [assimilate(): pl.pallas_call(assimilate_kernel, out_shape=jax.ShapeDtypeStruct((CELLS,...]
    all_gather x0 -> x1, blocking collectives: none -> 13.7 us  [body(): cube = lax.all_gather(plane, 'x', tiled=True)]
    all_to_all x1 -> x0, waiting for transfers between devices: 10.7 us -> none  [body(): lax.all_to_all(jnp.broadcast_to(plane, (4,) + plane.shape), 'x', 0, 0)]
    all_to_all x1 -> x0, starting transfers between devices: 5.7 us -> none  [body(): lax.all_to_all(jnp.broadcast_to(plane, (4,) + plane.shape), 'x', 0, 0)]
    ppermute x1, starting transfers between devices: 2.09 us -> 6.9 us  [body(): partner = lax.ppermute(cube, 'c', [(0, 1), (1, 0)])]
    concatenate x2, other arithmetic: 3.04 us -> 0.35 us  [the longest x1 0.27 us: body(): target = jnp.concatenate([target, target], axis=1)]
    select_n x0 -> x3, other arithmetic: none -> 1.97 us  [the longest x1 1.16 us: lon_halo(): outer = jnp.where(second, end, start)]
    reshape x1, local copies, waits for them, and re-layouts: 0.02 us -> 1.65 us  [body(): plane = plane[:, :SLOTS // 2, :].reshape(64 * SLOTS // 2, 128)]
  transfers between devices with their start and end apart: 7 -> 6, of which waited for: 4 -> 2; matrix products, arithmetic and copies ran while one was open for 12% -> 13% of each run, Pallas kernels for 0% -> 0%
where the time goes in v2:
time: 109 us
  starting transfers between devices  38.5 us (35%)
  Pallas kernels  22.1 us (20%)
  other arithmetic  15.9 us (15%)
  waiting for transfers between devices  14.5 us (13%)
  blocking collectives  13.7 us (13%)
  local copies, waits for them, and re-layouts  3.7 us (3%)
    pallas_call x1, Pallas kernels, assimilate(): pl.pallas_call(assimilate_kernel, out_shape=jax.ShapeDtypeStruct((CELLS,...  20.1 us
    all_to_all x1, starting transfers between devices, body(): plane = lax.all_to_all(send, PLANE, 0, 0)  14.9 us
    all_gather x1, blocking collectives, body(): cube = lax.all_gather(plane, 'x', tiled=True)  13.7 us
    ppermute x1, starting transfers between devices, lon_halo(): from_core = lax.ppermute(inner, 'c', [(0, 1), (1, 0)])  8.78 us
    ppermute x1, waiting for transfers between devices, lon_halo(): from_chip = lax.ppermute(outer, LON, pairs + [(b, a) for a, b in pairs])  7.99 us
    ppermute x1, starting transfers between devices, body(): partner = lax.ppermute(cube, 'c', [(0, 1), (1, 0)])  6.9 us
    select_n x3, other arithmetic, taper(): jnp.where(z <= 1.0, inner, jnp.where(z < 2.0, outer, jnp.float32(0.0)))  6.57 us
    all_to_all x1, waiting for transfers between devices, body(): plane = lax.all_to_all(send, PLANE, 0, 0)  6.51 us
  transfers between devices with their start and end apart: 6, of which 2 were waited for; matrix products, arithmetic and copies ran while one was open for 13% of the time, Pallas kernels for 0%

profile of v2, /device:TPU:1, one launch (start us, length us, event | category | flops | bytes accessed | tf_op | source)
XLA Modules:
  0.0 108.8 jit_solution(7323318521031149996)
XLA Ops:
  0.0 0.8 pad_maximum_fusion.7
  0.8 0.1 copy.22
  0.9 1.0 fusion.53
  1.9 1.3 %collective-permute-start.1 = (f32[2,8,1920]{2,1,0:T(8,128)S(1)}, f32[2,8,1920]{2,1,0:T(8,128)S(1)}, u32[]{:S(2)}, u32[]{:S(2)}) collective-permute-start(f32[2,8,1920]{2,1,0:T(8,128)S(1)} %get-tuple-element.28), channel_id=1, source_target_pairs={{32,0},{64,32},{96,64},{128,96},{160,128},{192,160},{224,192},{256... | collective-permute-start | bytes 368648 | tf_op jit(solution)/shard_map/ppermute | solution.py:298
  3.2 4.7 %collective-permute-start = (f32[2,8,1920]{2,1,0:T(8,128)S(1)}, f32[2,8,1920]{2,1,0:T(8,128)S(1)}, u32[]{:S(2)}, u32[]{:S(2)}) collective-permute-start(f32[2,8,1920]{2,1,0:T(8,128)S(1)} %get-tuple-element.29), channel_id=1, source_target_pairs={{0,32},{32,64},{64,96},{96,128},{128,160},{160,192},{192,224},{224... | collective-permute-start | bytes 368648 | tf_op jit(solution)/shard_map/ppermute | solution.py:297
  7.9 1.0 pad_maximum_fusion.1.mid
  8.8 0.1 iota_compare_fusion
  8.9 0.7 broadcast_compare_fusion
  9.6 1.6 %convert_reduce_fusion = s32[3,512]{1,0:T(4,128)S(1)} fusion(s32[3,512]{1,0:T(4,128)} %param.15, pred[512,512]{1,0:T(8,128)(4,1)S(1)} %iota_compare_fusion), kind=kLoop, calls=%fused_computation.1 | loop fusion | flops 3144192 | bytes 274432 | tf_op jit(solution)/shard_map/reduce_sum | solution.py:263
  11.3 0.8 select_reduce_fusion.1
  12.1 0.1 reshape.831
  12.2 0.8 add_select_fusion.5
  13.0 1.2 %broadcast_select_fusion = (f32[8,2,1920]{2,1,0:T(2,128)S(1)}, f32[8,2,1920]{2,1,0:T(2,128)S(1)}, f32[8,2,1920]{2,1,0:T(2,128)S(1)}) fusion(pred[]{:T(512)S(6)} %eq.77, f32[2,8,1920]{2,1,0:T(8,128)S(1)} %collective-permute-done.1.hi, f32[4,8,128]{2,1,0:T(8,128)S(1)} %pad.4, f32[4,8,1792]{2,1,0:T(8,128)} %param.11, f32[2,8,1920]{2,1,0:T(8,128)S(1)} %collective-permute-done.lo), kind=kLoop, calls=%fused_computation.86 | loop fusion | flops 215040 | bytes 860161 | tf_op jit(solution)/shard_map/jit(_where)/select_n | solution.py:306
  14.2 8.8 %collective-permute-start.2 = (f32[8,2,1920]{2,1,0:T(2,128)S(1)}, f32[8,2,1920]{2,1,0:T(2,128)S(1)}, u32[]{:S(2)}, u32[]{:S(2)}) collective-permute-start(f32[8,2,1920]{2,1,0:T(2,128)S(1)} %bitcast.28), channel_id=1, source_target_pairs={{0,1},{1,0},{2,3},{3,2},{4,5},{5,4},{6,7},{7,6},{8,9},{9,8},{10,11... | collective-permute-start | bytes 368648 | tf_op jit(solution)/shard_map/ppermute | solution.py:307
  23.0 2.0 %collective-permute-start.3 = (f32[8,2,1920]{2,1,0:T(2,128)S(1)}, f32[8,2,1920]{2,1,0:T(2,128)S(1)}, u32[]{:S(2)}, u32[]{:S(2)}) collective-permute-start(f32[8,2,1920]{2,1,0:T(2,128)S(1)} %get-tuple-element.25), channel_id=1, source_target_pairs={{1,2},{3,4},{5,6},{7,8},{9,10},{11,12},{13,14},{15,16},{17,18},{19... | collective-permute-start | bytes 368648 | tf_op jit(solution)/shard_map/ppermute | solution.py:309
  25.1 8.0 %collective-permute-done.3.from_chip = f32[8,2,1920]{2,1,0:T(2,128)S(1)} collective-permute-done((f32[8,2,1920]{2,1,0:T(2,128)S(1)}, f32[8,2,1920]{2,1,0:T(2,128)S(1)}, u32[]{:S(2)}, u32[]{:S(2)}) %collective-permute-start.3) | collective-permute-done | bytes 122912 | tf_op jit(solution)/shard_map/ppermute | solution.py:309
  33.1 2.1 %forecast.1 = (f32[14,32,128]{2,1,0:T(8,128)S(1)}, f32[64,8,128]{2,1,0:T(8,128)}) custom-call(s32[13]{0:T(128)S(1)} %pad_add_fusion.site_ref, f32[4,8,1920]{2,1,0:T(8,128)S(1)} %pad_maximum_fusion.1.mid, f32[2,8,1920]{2,1,0:T(8,128)S(1)} %collective-permute-done.lo, f32[2,8,1920]{2,1,0:T(8,128)S(1)} %collective-permute-done.1.hi, ...), custom_call_target="tpu_custom_call" | custom-call | tf_op jit(solution)/shard_map/forecast/pallas_call | solution.py:100
  35.3 0.1 select_reduce_fusion
  35.4 14.9 %all-to-all-start = ((f32[64,8,128]{2,1,0:T(8,128)}), f32[64,8,128]{2,1,0:T(8,128)}, u32[]{:S(2)}, u32[]{:S(2)}) async-start(f32[64,8,128]{2,1,0:T(8,128)} %get-tuple-element.17), calls=%async_computation | async-start | bytes 524288 | tf_op jit(solution)/shard_map/all_to_all | solution.py:344
  50.4 4.1 %fusion.6.rho_one = f32[1024,512]{1,0:T(8,128)S(1)} fusion(f32[512]{0:T(512)S(1)} %bitcast.43, s32[512]{0:T(512)S(1)} %bitcast.39, s32[1024]{0:T(1024)S(1)} %bitcast.45, s32[512]{0:T(512)S(1)} %bitcast.37, s32[1024]{0:T(1024)S(1)} %bitcast.46), kind=kLoop, calls=%fused_computation.14 | loop fusion | flops 24117248 | bytes 2111488 | tf_op jit(solution)/shard_map/jit(_where)/select_n | solution.py:47
  54.5 0.8 multiply_add_fusion
  55.3 1.3 %copy.23 = f32[3,512,64]{2,1,0:T(8,128)S(1)} copy(f32[3,512,64]{1,2,0:T(8,128)} %multiply_add_fusion) | data formatting | bytes 786432 | tf_op jit(solution)/shard_map/add | solution.py:341
  56.5 0.5 fusion.68
  57.0 6.5 %all-to-all-done = f32[64,8,128]{2,1,0:T(8,128)} async-done(((f32[64,8,128]{2,1,0:T(8,128)}), f32[64,8,128]{2,1,0:T(8,128)}, u32[]{:S(2)}, u32[]{:S(2)}) %all-to-all-start) | async-done | bytes 262176 | tf_op jit(solution)/shard_map/all_to_all | solution.py:344
  63.5 1.6 %reshape.833 = f32[384,128]{1,0:T(8,128)} reshape(f32[64,6,128]{2,1,0:T(8,128)} %bitcast.24) | data formatting | bytes 393216 | tf_op jit(solution)/shard_map/reshape | solution.py:345
  65.2 13.7 %all_gather.3.mine = f32[1536,128]{1,0:T(8,128)S(1)} all-gather(f32[384,128]{1,0:T(8,128)} %reshape.833), channel_id=1, replica_groups=mesh['x'=4,'yl'=4,'z'=8,'yh'=2,'c'=2] {'x'}, dimensions={0}, use_global_device_ids=true | all-gather | bytes 983040 | tf_op jit(solution)/shard_map/all_gather | solution.py:346
  78.9 6.9 %collective-permute-start.4 = (f32[1536,128]{1,0:T(8,128)S(1)}, f32[1536,128]{1,0:T(8,128)S(1)}, u32[]{:S(2)}, u32[]{:S(2)}) collective-permute-start(f32[1536,128]{1,0:T(8,128)S(1)} %all_gather.3.mine), channel_id=1, source_target_pairs={{0,1},{1,0},{2,3},{3,2},{4,5},{5,4},{6,7},{7,6},{8,9},{9,8},{10,11... | collective-permute-start | bytes 2359304 | tf_op jit(solution)/shard_map/ppermute | solution.py:347
  85.8 0.3 pad_maximum_fusion.target_ref
  86.1 2.1 %fusion.32.rho_two = f32[512,512]{1,0:T(8,128)S(1)} fusion(f32[512]{0:T(512)S(1)} %bitcast.42, s32[512]{0:T(512)S(1)} %bitcast.34, s32[512]{0:T(512)S(1)} %bitcast.36, s32[512]{0:T(512)S(1)} %bitcast.32, s32[512]{0:T(512)S(1)} %bitcast.30), kind=kLoop, calls=%fused_computation.49 | loop fusion | flops 12058624 | bytes 1058816 | tf_op jit(solution)/shard_map/jit(_where)/select_n | solution.py:47
  88.2 0.3 broadcast_in_dim.43.rinv_ref
  88.4 0.3 broadcast_in_dim.41.odd_ref
  88.7 20.1 %assimilate.1 = f32[32,1792]{1,0:T(8,128)} custom-call(s32[1536]{0:T(1024)S(1)} %reshape.830.row_ref, f32[14,32,128]{2,1,0:T(8,128)S(1)} %get-tuple-element.15.x_ref, f32[1536,128]{1,0:T(8,128)S(1)} %all_gather.3.mine, f32[1536,128]{1,0:T(8,128)S(1)} %collective-permute-done.4.theirs, f32[1536,128]{1,0:T(8,128)S(1)} %broadcast_in_dim.41.odd_ref, ...), custom_call_target="tpu_custom_call" | custom-call | tf_op jit(solution)/shard_map/assimilate/pallas_call | solution.py:242
  (36 shorter events, 0.3 us)
Async XLA Ops:
  0.0 35.2 %copy-start.1 = (s32[3,512]{1,0:T(4,128)S(1)}, s32[3,512]{1,0:T(4,128)}, u32[]{:S(2)}) copy-start(s32[3,512]{1,0:T(4,128)} %param.15) | copy-start | bytes 18436
  0.0 35.2 %copy-start.2 = (s32[3,512]{1,0:T(4,128)S(1)}, s32[3,512]{1,0:T(4,128)}, u32[]{:S(2)}) copy-start(s32[3,512]{1,0:T(4,128)} %param.16) | copy-start | bytes 18436
  0.0 35.3 %copy-start.5 = (s32[3,512]{1,0:T(4,128)S(1)}, s32[3,512]{1,0:T(4,128)}, u32[]{:S(2)}) copy-start(s32[3,512]{1,0:T(4,128)} %param.17) | copy-start | bytes 18436
  0.0 35.3 %copy-start.6 = (s32[8]{0:T(128)S(1)}, s32[8]{0:T(128)}, u32[]{:S(2)}) copy-start(s32[8]{0:T(128)} %param.18) | copy-start | bytes 100
  0.9 49.4 %copy-start.4 = (f32[3,512]{1,0:T(4,128)S(1)}, f32[3,512]{1,0:T(4,128)}, u32[]{:S(2)}) copy-start(f32[3,512]{1,0:T(4,128)} %param.20) | copy-start | bytes 18436
  1.9 11.1 %collective-permute-start.1 = (f32[2,8,1920]{2,1,0:T(8,128)S(1)}, f32[2,8,1920]{2,1,0:T(8,128)S(1)}, u32[]{:S(2)}, u32[]{:S(2)}) collective-permute-start(f32[2,8,1920]{2,1,0:T(8,128)S(1)} %get-tuple-element.28), channel_id=1, source_target_pairs={{32,0},{64,32},{96,64},{128,96},{160,128},{192,160},{224,192},{256... | collective-permute-start | bytes 368648 | tf_op jit(solution)/shard_map/ppermute | solution.py:298
  3.2 9.8 %collective-permute-start = (f32[2,8,1920]{2,1,0:T(8,128)S(1)}, f32[2,8,1920]{2,1,0:T(8,128)S(1)}, u32[]{:S(2)}, u32[]{:S(2)}) collective-permute-start(f32[2,8,1920]{2,1,0:T(8,128)S(1)} %get-tuple-element.29), channel_id=1, source_target_pairs={{0,32},{32,64},{64,96},{96,128},{128,160},{160,192},{192,224},{224... | collective-permute-start | bytes 368648 | tf_op jit(solution)/shard_map/ppermute | solution.py:297
  14.2 40.3 %copy-start = (f32[3,512,64]{1,2,0:T(8,128)S(1)}, f32[3,512,64]{1,2,0:T(8,128)}, u32[]{:S(2)}) copy-start(f32[3,512,64]{1,2,0:T(8,128)} %param.21) | copy-start | bytes 1179652
  14.2 40.3 %copy-start.3 = (f32[3,512]{1,0:T(4,128)S(1)}, f32[3,512]{1,0:T(4,128)}, u32[]{:S(2)}) copy-start(f32[3,512]{1,0:T(4,128)} %param.19) | copy-start | bytes 18436
  14.2 10.9 %collective-permute-start.2 = (f32[8,2,1920]{2,1,0:T(2,128)S(1)}, f32[8,2,1920]{2,1,0:T(2,128)S(1)}, u32[]{:S(2)}, u32[]{:S(2)}) collective-permute-start(f32[8,2,1920]{2,1,0:T(2,128)S(1)} %bitcast.28), channel_id=1, source_target_pairs={{0,1},{1,0},{2,3},{3,2},{4,5},{5,4},{6,7},{7,6},{8,9},{9,8},{10,11... | collective-permute-start | bytes 368648 | tf_op jit(solution)/shard_map/ppermute | solution.py:307
  23.0 10.1 %collective-permute-start.3 = (f32[8,2,1920]{2,1,0:T(2,128)S(1)}, f32[8,2,1920]{2,1,0:T(2,128)S(1)}, u32[]{:S(2)}, u32[]{:S(2)}) collective-permute-start(f32[8,2,1920]{2,1,0:T(2,128)S(1)} %get-tuple-element.25), channel_id=1, source_target_pairs={{1,2},{3,4},{5,6},{7,8},{9,10},{11,12},{13,14},{15,16},{17,18},{19... | collective-permute-start | bytes 368648 | tf_op jit(solution)/shard_map/ppermute | solution.py:309
  35.4 28.1 %all-to-all-start = ((f32[64,8,128]{2,1,0:T(8,128)}), f32[64,8,128]{2,1,0:T(8,128)}, u32[]{:S(2)}, u32[]{:S(2)}) async-start(f32[64,8,128]{2,1,0:T(8,128)} %get-tuple-element.17), calls=%async_computation | async-start | bytes 524288 | tf_op jit(solution)/shard_map/all_to_all | solution.py:344
  78.9 9.3 %collective-permute-start.4 = (f32[1536,128]{1,0:T(8,128)S(1)}, f32[1536,128]{1,0:T(8,128)S(1)}, u32[]{:S(2)}, u32[]{:S(2)}) collective-permute-start(f32[1536,128]{1,0:T(8,128)S(1)} %all_gather.3.mine), channel_id=1, source_target_pairs={{0,1},{1,0},{2,3},{3,2},{4,5},{5,4},{6,7},{7,6},{8,9},{9,8},{10,11... | collective-permute-start | bytes 2359304 | tf_op jit(solution)/shard_map/ppermute | solution.py:347

commit v3 on v2

v3 whole, which is shorter than its diff:
```python
import functools

import jax
import jax.numpy as jnp
from jax import lax
from jax.experimental import pallas as pl
from jax.experimental.pallas import tpu as pltpu
from jax.sharding import Mesh
from jax.sharding import PartitionSpec as P

LEV = 28
MEMBERS = 64
BATCH_GROUPS = 3
CAP = 4
NB = 512
CLAT = 4
CLON = 8
CELLS = CLAT * CLON
NLON = 256
N_LON = 32
WIDTH = LEV * MEMBERS
PACKED = WIDTH + 128
SLOTS = BATCH_GROUPS * CAP
ROWS = CELLS * LEV
OBS = BATCH_GROUPS * NB
HIGHEST = lax.Precision.HIGHEST
ADVECT = 0.2
STEP = 224
EVERY = 4

LAT = ("x", "yl")
LON = ("z", "yh", "c")
PLANE = ("yl", "z", "yh")


def taper(dist, radius):
    z = dist / radius
    inner = 1.0 - 5.0 / 3.0 * z**2 + 0.625 * z**3 + 0.5 * z**4 - 0.25 * z**5
    outside = jnp.maximum(z, 1.0)
    outer = (
        4.0
        - 5.0 * outside
        + 5.0 / 3.0 * outside**2
        + 0.625 * outside**3
        - 0.5 * outside**4
        + outside**5 / 12.0
        - 2.0 / (3.0 * outside)
    )
    return jnp.where(z <= 1.0, inner, jnp.where(z < 2.0, outer, jnp.float32(0.0)))


def rho_of(lat_a, lon_a, lat_b, lon_b, radius_b):
    dlat = jnp.abs(lat_a[:, None] - lat_b[None, :]).astype(jnp.float32)
    dlon = jnp.abs(lon_a[:, None] - lon_b[None, :])
    dlon = jnp.minimum(dlon, NLON - dlon).astype(jnp.float32)
    dist = jnp.sqrt(dlat * dlat + dlon * dlon)
    return taper(dist, radius_b[None, :])


def forecast_kernel(site_ref, mid, lo, hi, from_core, from_chip, x_ref, send_ref, grid, coef):
    grid[0:2, 0:8] = lo[...]
    grid[2:6, 0:8] = mid[...]
    grid[6:8, 0:8] = hi[...]
    grid[:, 8:16] = jnp.zeros((8, 8, PACKED), jnp.float32)
    winds = grid[1:7, :, WIDTH:PACKED]
    for n in range(3):
        coef[n] = jnp.broadcast_to(winds[:, :, n : n + 1], (6, 16, 128))
    second = site_ref[SLOTS] == 1
    core, chip = from_core[...], from_chip[...]
    for near, far, edge in (
        (8, 9, jnp.where(second, chip, core)),
        (15, 14, jnp.where(second, core, chip)),
    ):
        grid[1:7, near : near + 1, 0:WIDTH] = edge[0:6]
        grid[2:6, far : far + 1, 0:WIDTH] = edge[6:10]
        for n in range(3):
            for r in range(CLAT):
                lane = n * CLAT + r
                coef[n, 1 + r, near : near + 1, :] = jnp.broadcast_to(edge[10, :, lane : lane + 1], (1, 128))

    def step(v, nw, ew, ss):
        here, north, south = v[1:-1], v[2:], v[:-2]
        east_of = pltpu.roll(here, 15, 1)
        west_of = pltpu.roll(here, 1, 1)
        lap = north + south + east_of + west_of - 4.0 * here
        return here + ss * lap - ADVECT * (nw * (north - south) + ew * (east_of - west_of))

    for chunk in range(WIDTH // 128):
        lanes = slice(chunk * 128, chunk * 128 + 128)
        first = step(grid[:, :, lanes], coef[0], coef[1], coef[2])
        second = step(first, coef[0, 1:5], coef[1, 1:5], coef[2, 1:5])
        x_ref[chunk] = second[:, 0:8].reshape(CELLS, 128)

    lane = lax.broadcasted_iota(jnp.int32, (1, 128), 1)
    for pair in range(SLOTS // 2):
        halves = []
        for half in range(2):
            site = site_ref[2 * pair + half]
            cell = site // LEV
            level = site - cell * LEV
            row = x_ref[level // 2, pl.ds(cell, 1), :]
            swap = (level % 2) != half
            halves.append(jnp.where(swap, pltpu.roll(row, 64, 1), row))
        both = jnp.where(lane < 64, halves[0], halves[1])
        send_ref[:, pair, :] = jnp.broadcast_to(both, (send_ref.shape[0], 128))
    send_ref[:, SLOTS // 2 :, :] = jnp.zeros((send_ref.shape[0], 2, 128), jnp.float32)


def forecast(sites, mid, lo, hi, from_core, from_chip):
    vmem = pl.BlockSpec(memory_space=pltpu.VMEM)
    return pl.pallas_call(
        forecast_kernel,
        out_shape=(
            jax.ShapeDtypeStruct((WIDTH // 128, CELLS, 128), jnp.float32),
            pltpu.VMEM((64, 8, 128), jnp.float32),
        ),
        in_specs=[pl.BlockSpec(memory_space=pltpu.SMEM)] + [vmem] * 5,
        out_specs=(vmem, vmem),
        scratch_shapes=[
            pltpu.VMEM((8, 16, PACKED), jnp.float32),
            pltpu.VMEM((3, 6, 16, 128), jnp.float32),
        ],
        compiler_params=pltpu.CompilerParams(vmem_limit_bytes=8 << 20),
        name="forecast",
    )(sites, mid, lo, hi, from_core, from_chip)


def high(v):
    return v.astype(jnp.bfloat16).astype(jnp.float32)


def assimilate_kernel(
    row_ref, x_ref, mine, theirs, target_ref, rinv_ref, rho_own, rho_one_hbm, rho_two_hbm,
    out_ref, state, obs, every, rho_one, rho_two, anom_split, white_split, sems,
):
    first_copy = pltpu.make_async_copy(rho_one_hbm, rho_one, sems.at[0])
    second_copy = pltpu.make_async_copy(rho_two_hbm, rho_two, sems.at[1])
    first_copy.start()
    second_copy.start()
    left = lax.broadcasted_iota(jnp.int32, (1, 128), 1) < MEMBERS
    pairs = mine.shape[0]
    for offset, part in ((0, mine), (pairs, theirs)):
        both = part[...]
        swapped = pltpu.roll(both, MEMBERS, 1)
        every[offset : offset + pairs, :] = jnp.where(left, both, swapped)
        every[2 * pairs + offset : 3 * pairs + offset, :] = jnp.where(left, swapped, both)

    @pl.loop(0, OBS // 16)
    def _(n):
        base = pl.multiple_of(n * 16, 16)
        for i in range(16):
            obs[pl.ds(base + i, 1), :] = every[pl.ds(row_ref[base + i], 1), :]

    for level in range(0, LEV, 2):
        both = x_ref[level // 2]
        swapped = pltpu.roll(both, MEMBERS, 1)
        state[level * CELLS : (level + 1) * CELLS, :] = jnp.where(left, both, swapped)
        state[(level + 1) * CELLS : (level + 2) * CELLS, :] = jnp.where(left, swapped, both)

    row_id = lax.broadcasted_iota(jnp.int32, (MEMBERS, 128), 0)
    lane_id = lax.broadcasted_iota(jnp.int32, (MEMBERS, 128), 1)

    def updated(block, rho, k):
        dev = block - jnp.sum(block, axis=1, keepdims=True) * jnp.float32(1.0 / 128)
        dev_high = high(dev)
        dev = jnp.where(left, dev_high, dev - dev_high).astype(jnp.bfloat16)
        cov = jnp.dot(
            jnp.concatenate([dev, dev], axis=1),
            anom_split[k],
            preferred_element_type=jnp.float32,
        )
        cov = (cov.reshape((-1,) + rho.shape) * rho).reshape(-1, NB)
        cov_high = cov.astype(jnp.bfloat16)
        cov_low = (cov - cov_high.astype(jnp.float32)).astype(jnp.bfloat16)
        total = sum(
            lax.dot_general(
                part,
                white_split[k],
                (((1,), (1,)), ((), ())),
                preferred_element_type=jnp.float32,
            )
            for part in (cov_high, cov_low)
        )
        return block + (total + pltpu.roll(total, MEMBERS, 1))

    def update_state(k, piece):
        rows = slice(piece * STEP, piece * STEP + STEP)
        state[rows, :] = updated(state[rows, :], rho_own[k], k)

    for k in range(BATCH_GROUPS):
        here = slice(k * NB, k * NB + NB)
        prior = obs[here, :].T[:MEMBERS]
        anom = prior - jnp.sum(prior, axis=0, keepdims=True) * jnp.float32(1.0 / MEMBERS)
        innovation = target_ref[k] - prior
        anom_high = high(anom)
        anom_low = anom - anom_high
        anom_split[k] = jnp.concatenate(
            [anom_high, anom_high, anom_low, anom_low], axis=0
        ).astype(jnp.bfloat16)
        work = lax.dot_general(
            anom * rinv_ref[k],
            jnp.concatenate([anom, innovation], axis=0),
            (((1,), (1,)), ((), ())),
            precision=HIGHEST,
            preferred_element_type=jnp.float32,
        )
        work = jnp.where(row_id == lane_id, work + jnp.float32(MEMBERS - 1), work)
        for p in range(0, MEMBERS, 4):
            if k and p % (4 * EVERY) == 0 and p // (4 * EVERY) < ROWS // STEP:
                update_state(k - 1, p // (4 * EVERY))
            cols = [jnp.broadcast_to(work[:, p + t : p + t + 1], (MEMBERS, 128)) for t in range(4)]
            rows = [work[p + t : p + t + 1, :] for t in range(4)]
            e = [[cols[t][p + r : p + r + 1] for t in range(4)] for r in range(4)]
            det = 1.0 / (e[0][0] * e[1][1] - e[0][1] * e[1][0])
            top0 = (e[1][1] * rows[0] - e[0][1] * rows[1]) * det
            top1 = (e[0][0] * rows[1] - e[1][0] * rows[0]) * det
            u0 = [(e[1][1] * e[0][t] - e[0][1] * e[1][t]) * det for t in (2, 3)]
            u1 = [(e[0][0] * e[1][t] - e[1][0] * e[0][t]) * det for t in (2, 3)]
            s = [[e[r][t] - e[r][0] * u0[t - 2] - e[r][1] * u1[t - 2] for t in (2, 3)] for r in (2, 3)]
            low = [rows[r] - e[r][0] * top0 - e[r][1] * top1 for r in (2, 3)]
            det = 1.0 / (s[0][0] * s[1][1] - s[0][1] * s[1][0])
            new2 = (s[1][1] * low[0] - s[0][1] * low[1]) * det
            new3 = (s[0][0] * low[1] - s[1][0] * low[0]) * det
            new0 = top0 - u0[0] * new2 - u0[1] * new3
            new1 = top1 - u1[0] * new2 - u1[1] * new3
            fresh = (new0, new1, new2, new3)
            for t in range(4):
                work = work - cols[t] * fresh[t]
            for t in range(4):
                work = jnp.where(row_id == p + t, fresh[t], work)
        weights = pltpu.roll(work, MEMBERS, 1)[:, :MEMBERS]
        white = innovation - lax.dot_general(
            weights,
            anom,
            (((0,), (0,)), ((), ())),
            precision=HIGHEST,
            preferred_element_type=jnp.float32,
        )
        white_high = high(white)
        white_split[k] = jnp.concatenate([white_high, white - white_high], axis=0).astype(jnp.bfloat16)

        if k < BATCH_GROUPS - 1:
            (first_copy, second_copy)[k].wait()
            rho = (rho_one, rho_two)[k]
            for n in range(BATCH_GROUPS - 1 - k):
                rows = slice((k + 1 + n) * NB, (k + 2 + n) * NB)
                obs[rows, :] = updated(obs[rows, :], rho[n * NB : n * NB + NB, :], k)
    for piece in range(ROWS // STEP):
        update_state(BATCH_GROUPS - 1, piece)

    for level in range(0, LEV, 2):
        low = state[level * CELLS : (level + 1) * CELLS, :]
        upper = state[(level + 1) * CELLS : (level + 2) * CELLS, :]
        out_ref[:, level * MEMBERS : (level + 2) * MEMBERS] = jnp.where(left, low, upper)


def assimilate(row, x, mine, theirs, target, rinv, rho_own, rho_one, rho_two):
    vmem = pl.BlockSpec(memory_space=pltpu.VMEM)
    hbm = pl.BlockSpec(memory_space=pltpu.HBM)
    return pl.pallas_call(
        assimilate_kernel,
        out_shape=jax.ShapeDtypeStruct((CELLS, WIDTH), jnp.float32),
        in_specs=[pl.BlockSpec(memory_space=pltpu.SMEM)] + [vmem] * 6 + [hbm] * 2,
        out_specs=vmem,
        scratch_shapes=[
            pltpu.VMEM((ROWS, 128), jnp.float32),
            pltpu.VMEM((OBS, 128), jnp.float32),
            pltpu.VMEM((4 * mine.shape[0], 128), jnp.float32),
            pltpu.VMEM(rho_one.shape, jnp.float32),
            pltpu.VMEM(rho_two.shape, jnp.float32),
            pltpu.VMEM((BATCH_GROUPS, 4 * MEMBERS, NB), jnp.bfloat16),
            pltpu.VMEM((BATCH_GROUPS, 2 * MEMBERS, NB), jnp.bfloat16),
            pltpu.SemaphoreType.DMA((2,)),
        ],
        compiler_params=pltpu.CompilerParams(vmem_limit_bytes=32 << 20),
        name="assimilate",
    )(row, x, mine, theirs, target, rinv, rho_own, rho_one, rho_two)


def slots(lat_tile, lon_tile, owner, site):
    order = jnp.arange(NB, dtype=jnp.int32)
    same = (owner[:, :, None] == owner[:, None, :]) & (order[None, :] < order[:, None])
    rank = jnp.sum(same.astype(jnp.int32), axis=2)
    slot = jnp.arange(BATCH_GROUPS, dtype=jnp.int32)[:, None] * CAP + rank
    mine = owner == lat_tile * N_LON + lon_tile
    chosen = mine[:, None, :] & (rank[:, None, :] == jnp.arange(CAP, dtype=jnp.int32)[:, None])
    sites = jnp.sum(jnp.where(chosen, site[:, None, :], 0), axis=2).reshape(SLOTS)
    lat, lon = owner // N_LON, owner % N_LON
    x, yl = lat // 4, lat % 4
    z, yh, c = lon // 4, lon // 2 % 2, lon % 2
    other = jnp.where(c == lon_tile % 2, 0, 1)
    row = ((other * 4 + x) * 64 + (yl * 8 + z) * 2 + yh) * (SLOTS // 2) + slot // 2
    row = row + slot % 2 * (N_LON * 16 * SLOTS // 2)
    return jnp.append(sites, lon_tile % 2), row.reshape(OBS)


def tapers(lat_tile, lon_tile, owner, site, obs_class, cutoff_table, scale):
    cell = site // LEV
    glat = owner // N_LON * CLAT + cell // CLON
    glon = owner % N_LON * CLON + cell % CLON
    classes = jnp.arange(cutoff_table.shape[0], dtype=jnp.int32)
    match = (obs_class[:, :, None] == classes).astype(jnp.int32)
    radius = jnp.sum(match * cutoff_table, axis=2).astype(jnp.float32)
    rho_one = rho_of(glat[1:].reshape(-1), glon[1:].reshape(-1), glat[0], glon[0], radius[0]) * scale[0]
    rho_two = rho_of(glat[2], glon[2], glat[1], glon[1], radius[1]) * scale[1]
    local = jnp.arange(CELLS, dtype=jnp.int32)
    cell_lat = lat_tile * CLAT + local // CLON
    cell_lon = lon_tile * CLON + local % CLON
    rho_own = jnp.stack(
        [rho_of(cell_lat, cell_lon, glat[k], glon[k], radius[k]) * scale[k] for k in range(BATCH_GROUPS)]
    )
    return rho_one, rho_two, rho_own


def lat_halo(block):
    forward = [(i, i + 1) for i in range(15)]
    backward = [(b, a) for a, b in forward]
    low = lax.ppermute(block[CLAT - 2 :], LAT, forward)
    high = lax.ppermute(block[:2], LAT, backward)
    return low, high


def lon_halo(lo, mid, hi, winds):
    def edge(near, far):
        fields = jnp.pad(winds[:, near].T.reshape(1, 3 * CLAT), ((0, 0), (0, WIDTH - 3 * CLAT)))
        parts = [lo[1:, near, :WIDTH], mid[:, near, :WIDTH], hi[:1, near, :WIDTH], mid[:, far, :WIDTH], fields]
        return jnp.concatenate(parts, axis=0)[:, None, :]

    second = lax.axis_index("c") == 1
    start, end = edge(0, 1), edge(CLON - 1, CLON - 2)
    inner = jnp.where(second, start, end)
    outer = jnp.where(second, end, start)
    from_core = lax.ppermute(inner, "c", [(0, 1), (1, 0)])
    pairs = [(i, (i + 1) % N_LON) for i in range(1, N_LON, 2)]
    from_chip = lax.ppermute(outer, LON, pairs + [(b, a) for a, b in pairs])
    return from_core, from_chip


def body(
    ensemble,
    northward_wind,
    eastward_wind,
    spreading_strength,
    owner,
    site,
    obs_class,
    cutoff_table,
    obs_value,
    obs_var,
    obs_noise,
):
    lat_tile = lax.axis_index("x") * 4 + lax.axis_index("yl")
    lon_tile = lax.axis_index("z") * 4 + lax.axis_index("yh") * 2 + lax.axis_index("c")
    winds = jnp.stack([northward_wind, eastward_wind, spreading_strength], axis=2)
    mid = jnp.concatenate([ensemble, jnp.pad(winds, ((0, 0), (0, 0), (0, 125)))], axis=2)
    lo, hi = lat_halo(mid)
    from_core, from_chip = lon_halo(lo, mid, hi, winds)
    sites, row = slots(lat_tile, lon_tile, owner, site)
    state, send = forecast(sites, mid, lo, hi, from_core, from_chip)
    send, owner, site, obs_class, obs_var, obs_value, obs_noise = lax.optimization_barrier(
        (send, owner, site, obs_class, obs_var, obs_value, obs_noise)
    )
    rinv = (1.0 / obs_var)[:, None, :]
    rho_one, rho_two, rho_own = tapers(
        lat_tile, lon_tile, owner, site, obs_class, cutoff_table, rinv / (MEMBERS - 1)
    )
    target = obs_value[:, None, :] + jnp.sqrt(obs_var)[:, None, :] * jnp.swapaxes(obs_noise, 1, 2)
    plane = lax.all_to_all(send, PLANE, 0, 0)
    plane = plane[:, : SLOTS // 2, :].reshape(64 * SLOTS // 2, 128)
    cube = lax.all_gather(plane, "x", tiled=True)
    partner = lax.ppermute(cube, "c", [(0, 1), (1, 0)])
    out = assimilate(row, state, cube, partner, target, rinv, rho_own, rho_one, rho_two)
    return out.reshape(CLAT, CLON, WIDTH)


def solution(mesh):
    split = Mesh(mesh.devices.reshape(4, 4, 8, 2, 2), LAT + LON)
    tile = P(LAT, LON)
    return jax.shard_map(
        body,
        mesh=split,
        in_specs=(P(LAT, LON, None), tile, tile, tile) + (P(),) * 7,
        out_specs=P(LAT, LON, None),
        check_vma=False,
    )
```

time: 109 us -> 99.7 us (0.915)
  waiting for transfers between devices: 14.5 us -> 8.8 us
  other arithmetic: 15.9 us -> 12.9 us
  starting transfers between devices: 38.5 us -> 41.4 us
  Pallas kernels: 22.1 us -> 19.6 us
    ppermute x1, waiting for transfers between devices: 7.99 us -> 0.01 us  [lon_halo(): from_chip = lax.ppermute(outer, LON, pairs + [(b, a) for a, b in pairs])]
    select_n x5 -> x0, other arithmetic: 7.38 us -> none  [the longest x3 6.57 us: taper(): jnp.where(z <= 1.0, inner, jnp.where(z < 2.0, outer, jnp.float32(0.0)))]
    ppermute x1, starting transfers between devices: 2.01 us -> 8.73 us  [lon_halo(): from_chip = lax.ppermute(outer, LON, pairs + [(b, a) for a, b in pairs])]
    mul x0 -> x3, other arithmetic: none -> 6.69 us  [the longest x1 4.13 us: tapers(): rho_of(glat[1:].reshape(-1), glon[1:].reshape(-1), glat[0], glon[0], radi...]
    all_to_all x1, starting transfers between devices: 14.9 us -> 9.59 us  [body(): plane = lax.all_to_all(send, PLANE, 0, 0)]
    pallas_call x1, Pallas kernels: 20.1 us -> 17.5 us  [assimilate(): pl.pallas_call(assimilate_kernel, out_shape=jax.ShapeDtypeStruct((CELLS,...]
    unnamed x17 -> x22, local copies, waits for them, and re-layouts: 0.04 us -> 2.29 us
    reshape x1, local copies, waits for them, and re-layouts: 1.65 us -> 0.02 us  [body(): plane = plane[:, :SLOTS // 2, :].reshape(64 * SLOTS // 2, 128)]
where the time goes in v3:
time: 99.7 us; the launch traced here: 99.1 us
  starting transfers between devices  41.4 us (42%)
  Pallas kernels  19.6 us (20%)
  other arithmetic  12.9 us (13%)
  blocking collectives  12.8 us (13%)
  waiting for transfers between devices  8.8 us (9%)
  local copies, waits for them, and re-layouts  3.03 us (3%)
    pallas_call x1, Pallas kernels, assimilate(): pl.pallas_call(assimilate_kernel, out_shape=jax.ShapeDtypeStruct((CELLS,...  17.5 us
    all_gather x1, blocking collectives, body(): cube = lax.all_gather(plane, 'x', tiled=True)  12.8 us
    ppermute x1, starting transfers between devices, lon_halo(): from_core = lax.ppermute(inner, 'c', [(0, 1), (1, 0)])  9.66 us
    all_to_all x1, starting transfers between devices, body(): plane = lax.all_to_all(send, PLANE, 0, 0)  9.59 us
    ppermute x1, starting transfers between devices, lon_halo(): from_chip = lax.ppermute(outer, LON, pairs + [(b, a) for a, b in pairs])  8.73 us
    all_to_all x1, waiting for transfers between devices, body(): plane = lax.all_to_all(send, PLANE, 0, 0)  7.97 us
    ppermute x1, starting transfers between devices, body(): partner = lax.ppermute(cube, 'c', [(0, 1), (1, 0)])  7.5 us
    ppermute x1, starting transfers between devices, lat_halo(): low = lax.ppermute(block[CLAT - 2:], LAT, forward)  4.65 us
  transfers between devices with their start and end apart: 6, of which 2 were waited for; matrix products, arithmetic and copies ran while one was open for 13% of the time, Pallas kernels for 0%

profile of v3, /device:TPU:1, one launch (start us, length us, event | category | flops | bytes accessed | tf_op | source)
XLA Modules:
  0.0 99.1 jit_solution(18172871351602399270)
XLA Ops:
  0.0 0.8 pad_maximum_fusion.1
  0.8 0.1 copy.27
  0.9 1.0 select_maximum_fusion.mid
  1.9 1.3 %collective-permute-start.1 = (f32[2,8,1920]{2,1,0:T(8,128)S(1)}, f32[2,8,1920]{2,1,0:T(8,128)S(1)}, u32[]{:S(2)}, u32[]{:S(2)}) collective-permute-start(f32[2,8,1920]{2,1,0:T(8,128)S(1)} %get-tuple-element.25), channel_id=1, source_target_pairs={{32,0},{64,32},{96,64},{128,96},{160,128},{192,160},{224,192},{256... | collective-permute-start | bytes 368648 | tf_op jit(solution)/shard_map/ppermute | solution.py:319
  3.2 4.7 %collective-permute-start = (f32[2,8,1920]{2,1,0:T(8,128)S(1)}, f32[2,8,1920]{2,1,0:T(8,128)S(1)}, u32[]{:S(2)}, u32[]{:S(2)}) collective-permute-start(f32[2,8,1920]{2,1,0:T(8,128)S(1)} %get-tuple-element.26), channel_id=1, source_target_pairs={{0,32},{32,64},{64,96},{96,128},{128,160},{160,192},{192,224},{224... | collective-permute-start | bytes 368648 | tf_op jit(solution)/shard_map/ppermute | solution.py:318
  7.9 0.1 iota_compare_fusion
  8.0 0.7 broadcast_compare_fusion
  8.7 1.6 %convert_reduce_fusion = s32[3,512]{1,0:T(4,128)S(1)} fusion(s32[3,512]{1,0:T(4,128)} %param.15, pred[512,512]{1,0:T(8,128)(4,1)S(1)} %iota_compare_fusion), kind=kLoop, calls=%fused_computation.1 | loop fusion | flops 3144192 | bytes 274432 | tf_op jit(solution)/shard_map/reduce_sum | solution.py:283
  10.4 0.8 fusion.143
  11.2 0.8 select_reduce_fusion.1
  12.0 0.1 copy.33
  12.1 0.1 reshape.1160
  12.2 0.1 copy.32
  12.3 0.1 reshape.1159
  12.4 0.1 reshape.1157
  12.5 1.1 %slice_dynamic-update-slice_fusion.1 = (f32[11,1,1792]{2,1,0:T(1,128)S(1)}, f32[11,1,1792]{2,1,0:T(1,128)S(1)}) fusion(f32[11,1,1792]{2,1,0:T(1,128)S(1)} %get-tuple-element.35, f32[4,8,1792]{2,1,0:T(8,128)} %param.11, f32[11,1,1792]{2,1,0:T(1,128)S(1)} %get-tuple-element.36), kind=kLoop, calls=%fused_computation.191 | loop fusion | bytes 114688
  13.7 1.1 %slice_dynamic-update-slice_fusion = (f32[11,1,1792]{2,1,0:T(1,128)S(1)}, f32[11,1,1792]{2,1,0:T(1,128)S(1)}) fusion(f32[11,1,1792]{2,1,0:T(1,128)S(1)} %get-tuple-element.33, f32[4,8,1792]{2,1,0:T(8,128)} %param.11, f32[11,1,1792]{2,1,0:T(1,128)S(1)} %get-tuple-element.34), kind=kLoop, calls=%fused_computation.190 | loop fusion | bytes 114688
  14.8 0.1 broadcast_select_fusion
  14.9 8.7 %collective-permute-start.3 = (f32[11,1,1792]{2,1,0:T(1,128)S(1)}, f32[11,1,1792]{2,1,0:T(1,128)S(1)}, u32[]{:S(2)}, u32[]{:S(2)}) collective-permute-start(f32[11,1,1792]{2,1,0:T(1,128)S(1)} %get-tuple-element.31), channel_id=1, source_target_pairs={{1,2},{3,4},{5,6},{7,8},{9,10},{11,12},{13,14},{15,16},{17,18},{19... | collective-permute-start | bytes 236552 | tf_op jit(solution)/shard_map/ppermute | solution.py:335
  23.7 9.7 %collective-permute-start.2 = (f32[11,1,1792]{2,1,0:T(1,128)S(1)}, f32[11,1,1792]{2,1,0:T(1,128)S(1)}, u32[]{:S(2)}, u32[]{:S(2)}) collective-permute-start(f32[11,1,1792]{2,1,0:T(1,128)S(1)} %get-tuple-element.32), channel_id=1, source_target_pairs={{0,1},{1,0},{2,3},{3,2},{4,5},{5,4},{6,7},{7,6},{8,9},{9,8},{10,11... | collective-permute-start | bytes 236552 | tf_op jit(solution)/shard_map/ppermute | solution.py:333
  33.3 0.1 pad_add_fusion.site_ref
  33.4 0.8 collective-permute-done.2.from_core
  34.2 2.2 %forecast.1 = (f32[14,32,128]{2,1,0:T(8,128)S(1)}, f32[64,8,128]{2,1,0:T(8,128)}) custom-call(s32[13]{0:T(128)S(1)} %pad_add_fusion.site_ref, f32[4,8,1920]{2,1,0:T(8,128)S(1)} %select_maximum_fusion.mid, f32[2,8,1920]{2,1,0:T(8,128)S(1)} %collective-permute-done.lo, f32[2,8,1920]{2,1,0:T(8,128)S(1)} %collective-permute-done.1.hi, ...), custom_call_target="tpu_custom_call" | custom-call | tf_op jit(solution)/shard_map/forecast/pallas_call | solution.py:111
  36.5 0.1 select_reduce_fusion
  36.6 9.6 %all-to-all-start = ((f32[64,8,128]{2,1,0:T(8,128)}), f32[64,8,128]{2,1,0:T(8,128)S(1)}, u32[]{:S(2)}, u32[]{:S(2)}) async-start(f32[64,8,128]{2,1,0:T(8,128)} %get-tuple-element.16), calls=%async_computation | async-start | bytes 524288 | tf_op jit(solution)/shard_map/all_to_all | solution.py:368
  46.3 4.1 %fusion.7.rho_one_hbm = f32[1024,512]{1,0:T(8,128)S(1)} fusion(f32[512]{0:T(512)S(1)} %bitcast.55, f32[512]{0:T(512)S(1)} %bitcast.53, s32[512]{0:T(512)S(1)} %bitcast.51, s32[1024]{0:T(1024)S(1)} %bitcast.58, s32[512]{0:T(512)S(1)} %bitcast.49, s32[1024]{0:T(1024)S(1)} %bitcast.57), kind=kLoop, calls=%fused_computation.15 | loop fusion | flops 24641536 | bytes 2113536 | tf_op jit(solution)/shard_map/mul | solution.py:304
  50.5 0.5 fusion.69
  51.0 8.0 %all-to-all-done = f32[64,8,128]{2,1,0:T(8,128)S(1)} async-done(((f32[64,8,128]{2,1,0:T(8,128)}), f32[64,8,128]{2,1,0:T(8,128)S(1)}, u32[]{:S(2)}, u32[]{:S(2)}) %all-to-all-start) | async-done | bytes 262176 | tf_op jit(solution)/shard_map/all_to_all | solution.py:368
  59.0 12.8 %all_gather.3.mine = f32[1536,128]{1,0:T(8,128)S(1)} all-gather(f32[384,128]{1,0:T(8,128)S(1)} %reshape.1161), channel_id=1, replica_groups=mesh['x'=4,'yl'=4,'z'=8,'yh'=2,'c'=2] {'x'}, dimensions={0}, use_global_device_ids=true | all-gather | bytes 983040 | tf_op jit(solution)/shard_map/all_gather | solution.py:370
  71.7 7.5 %collective-permute-start.4 = (f32[1536,128]{1,0:T(8,128)S(1)}, f32[1536,128]{1,0:T(8,128)S(1)}, u32[]{:S(2)}, u32[]{:S(2)}) collective-permute-start(f32[1536,128]{1,0:T(8,128)S(1)} %all_gather.3.mine), channel_id=1, source_target_pairs={{0,1},{1,0},{2,3},{3,2},{4,5},{5,4},{6,7},{7,6},{8,9},{9,8},{10,11... | collective-permute-start | bytes 2359304 | tf_op jit(solution)/shard_map/ppermute | solution.py:371
  79.3 2.1 %fusion.34.rho_two_hbm = f32[512,512]{1,0:T(8,128)S(1)} fusion(f32[512]{0:T(512)S(1)} %bitcast.48, f32[512]{0:T(512)S(1)} %bitcast.46, s32[512]{0:T(512)S(1)} %bitcast.44, s32[512]{0:T(512)S(1)} %bitcast.42, s32[512]{0:T(512)S(1)} %bitcast.40, s32[512]{0:T(512)S(1)} %bitcast.38), kind=kLoop, calls=%fused_computation.51 | loop fusion | flops 12320768 | bytes 1060864 | tf_op jit(solution)/shard_map/mul | solution.py:305
  81.4 17.5 %assimilate.1 = f32[32,1792]{1,0:T(8,128)} custom-call(s32[1536]{0:T(1024)S(1)} %reshape.1156.row_ref, f32[14,32,128]{2,1,0:T(8,128)S(1)} %get-tuple-element.14.x_ref, f32[1536,128]{1,0:T(8,128)S(1)} %all_gather.3.mine, f32[1536,128]{1,0:T(8,128)S(1)} %collective-permute-done.4.theirs, f32[3,64,512]{2,1,0:T(8,128)S(1)} %add_bitcast_fusion.target_ref, ...), custom_call_target="tpu_custom_call" | custom-call | tf_op jit(solution)/shard_map/assimilate/pallas_call | solution.py:260
  (41 shorter events, 0.4 us)
Async XLA Ops:
  0.0 36.4 %copy-start.1 = (s32[3,512]{1,0:T(4,128)S(1)}, s32[3,512]{1,0:T(4,128)}, u32[]{:S(2)}) copy-start(s32[3,512]{1,0:T(4,128)} %param.15) | copy-start | bytes 18436
  0.0 36.4 %copy-start.2 = (s32[3,512]{1,0:T(4,128)S(1)}, s32[3,512]{1,0:T(4,128)}, u32[]{:S(2)}) copy-start(s32[3,512]{1,0:T(4,128)} %param.16) | copy-start | bytes 18436
  0.0 46.3 %copy-start.5 = (f32[3,512]{1,0:T(4,128)S(1)}, f32[3,512]{1,0:T(4,128)}, u32[]{:S(2)}) copy-start(f32[3,512]{1,0:T(4,128)} %param.20) | copy-start | bytes 18436
  0.0 36.5 %copy-start.4 = (s32[3,512]{1,0:T(4,128)S(1)}, s32[3,512]{1,0:T(4,128)}, u32[]{:S(2)}) copy-start(s32[3,512]{1,0:T(4,128)} %param.17) | copy-start | bytes 18436
  0.0 36.5 %copy-start.6 = (s32[8]{0:T(128)S(1)}, s32[8]{0:T(128)}, u32[]{:S(2)}) copy-start(s32[8]{0:T(128)} %param.18) | copy-start | bytes 100
  1.9 11.8 %collective-permute-start.1 = (f32[2,8,1920]{2,1,0:T(8,128)S(1)}, f32[2,8,1920]{2,1,0:T(8,128)S(1)}, u32[]{:S(2)}, u32[]{:S(2)}) collective-permute-start(f32[2,8,1920]{2,1,0:T(8,128)S(1)} %get-tuple-element.25), channel_id=1, source_target_pairs={{32,0},{64,32},{96,64},{128,96},{160,128},{192,160},{224,192},{256... | collective-permute-start | bytes 368648 | tf_op jit(solution)/shard_map/ppermute | solution.py:319
  3.2 9.3 %collective-permute-start = (f32[2,8,1920]{2,1,0:T(8,128)S(1)}, f32[2,8,1920]{2,1,0:T(8,128)S(1)}, u32[]{:S(2)}, u32[]{:S(2)}) collective-permute-start(f32[2,8,1920]{2,1,0:T(8,128)S(1)} %get-tuple-element.26), channel_id=1, source_target_pairs={{0,32},{32,64},{64,96},{96,128},{128,160},{160,192},{192,224},{224... | collective-permute-start | bytes 368648 | tf_op jit(solution)/shard_map/ppermute | solution.py:318
  14.9 18.5 %collective-permute-start.3 = (f32[11,1,1792]{2,1,0:T(1,128)S(1)}, f32[11,1,1792]{2,1,0:T(1,128)S(1)}, u32[]{:S(2)}, u32[]{:S(2)}) collective-permute-start(f32[11,1,1792]{2,1,0:T(1,128)S(1)} %get-tuple-element.31), channel_id=1, source_target_pairs={{1,2},{3,4},{5,6},{7,8},{9,10},{11,12},{13,14},{15,16},{17,18},{19... | collective-permute-start | bytes 236552 | tf_op jit(solution)/shard_map/ppermute | solution.py:335
  23.7 10.6 %collective-permute-start.2 = (f32[11,1,1792]{2,1,0:T(1,128)S(1)}, f32[11,1,1792]{2,1,0:T(1,128)S(1)}, u32[]{:S(2)}, u32[]{:S(2)}) collective-permute-start(f32[11,1,1792]{2,1,0:T(1,128)S(1)} %get-tuple-element.32), channel_id=1, source_target_pairs={{0,1},{1,0},{2,3},{3,2},{4,5},{5,4},{6,7},{7,6},{8,9},{9,8},{10,11... | collective-permute-start | bytes 236552 | tf_op jit(solution)/shard_map/ppermute | solution.py:333
  36.6 22.3 %all-to-all-start = ((f32[64,8,128]{2,1,0:T(8,128)}), f32[64,8,128]{2,1,0:T(8,128)S(1)}, u32[]{:S(2)}, u32[]{:S(2)}) async-start(f32[64,8,128]{2,1,0:T(8,128)} %get-tuple-element.16), calls=%async_computation | async-start | bytes 524288 | tf_op jit(solution)/shard_map/all_to_all | solution.py:368
  46.3 32.9 %copy-start = (f32[3,512,64]{1,2,0:T(8,128)S(1)}, f32[3,512,64]{1,2,0:T(8,128)}, u32[]{:S(2)}) copy-start(f32[3,512,64]{1,2,0:T(8,128)} %param.21) | copy-start | bytes 1179652
  46.3 32.9 %copy-start.3 = (f32[3,512]{1,0:T(4,128)S(1)}, f32[3,512]{1,0:T(4,128)}, u32[]{:S(2)}) copy-start(f32[3,512]{1,0:T(4,128)} %param.19) | copy-start | bytes 18436
  71.7 9.7 %collective-permute-start.4 = (f32[1536,128]{1,0:T(8,128)S(1)}, f32[1536,128]{1,0:T(8,128)S(1)}, u32[]{:S(2)}, u32[]{:S(2)}) collective-permute-start(f32[1536,128]{1,0:T(8,128)S(1)} %all_gather.3.mine), channel_id=1, source_target_pairs={{0,1},{1,0},{2,3},{3,2},{4,5},{5,4},{6,7},{7,6},{8,9},{9,8},{10,11... | collective-permute-start | bytes 2359304 | tf_op jit(solution)/shard_map/ppermute | solution.py:371
